TPU v7x, 32 devices: a whole 2x2x4 slice. The times are simulated.
32 devices in a mesh: tm: 16 (over z, x, core), space: 2 (over y).
Axes of the slice: x: 2, y: 2, z: 4, core: 2. Of those that a mesh axis runs over, the one named last changes fastest.
Arguments:
- stream: bfloat16 [32, 12, 40, 2240], P('tm', 'space'), may hold values from -6 to 6
- queries: bfloat16 [32, 12, 40, 2240], P('tm', 'space'), may hold values from -6 to 6
- keys: bfloat16 [32, 12, 40, 2240], P('tm', 'space'), may hold values from -6 to 6
- values: bfloat16 [32, 12, 40, 2240], P('tm', 'space'), may hold values from -6 to 6
- state_in: float32 [20, 112, 112], replicated, may hold values from -120 to 120
- keysum_in: float32 [20, 112], replicated, may hold values from 100 to 1000
- attn_gate: float32 [2240], replicated, may hold values from 2 to 20
- ffn_shift: float32 [2240], replicated, may hold values from -3 to 3
- ffn_scale: float32 [2240], replicated, may hold values from -3 to 3
- w_up: bfloat16 [2240, 5600], P('tm'), may hold values from -0.125 to 0.125
- conv_weight: float32 [3, 3, 5600], replicated, may hold values from -2 to 2
- conv_bias: float32 [5600], replicated, may hold values from -3 to 3
Outputs:
- mixed: bfloat16 [32, 12, 40, 2240], P('tm', 'space')
- hidden: bfloat16 [32, 12, 40, 2800], P('tm', 'space')
All inputs are finite; a program needn't handle non-finite values.
Results may differ from a plain program's by a relative error of at most 0.0076.
Values may be sent and summed in bfloat16 or wider, within the bound.
No kernel may reach another device: no remote copies, remote signals or barrier semaphores. Data moves between devices by JAX's collectives and lax.ppermute only.
A program may use at most 192 MiB of HBM per device.

v0:
```python
import jax
import jax.numpy as jnp
from jax import lax
from jax.sharding import PartitionSpec as P

EPS = 1e-06


def entering(array, axis, combine, identity):
    peers, mine = (lax.axis_size(axis), lax.axis_index(axis))
    everything = jax.tree.map(lambda part: lax.all_gather(part, axis), array)
    start = jax.tree.map(
        lambda part, zero: jnp.broadcast_to(jnp.asarray(zero, part.dtype), part.shape),
        array,
        identity,
    )

    def step(k, before):
        reached = k < mine
        new = combine(before, jax.tree.map(lambda part: part[k], everything))
        return jax.tree.map(lambda a, b: jnp.where(reached, a, b), new, before)

    return lax.fori_loop(0, peers, step, start)


def with_halo(cells, sides, width):
    for axis, dim in sides:
        count = lax.axis_size(axis)
        ends = count - 1
        head = lax.slice_in_dim(cells, 0, width, axis=dim)
        tail = lax.slice_in_dim(cells, cells.shape[dim] - width, cells.shape[dim], axis=dim)
        cells = jnp.concatenate(
            [
                lax.ppermute(tail, axis, [(i, (i + 1) % count) for i in range(ends)]),
                cells,
                lax.ppermute(head, axis, [((i + 1) % count, i) for i in range(ends)]),
            ],
            axis=dim,
        )
    return cells


def add_totals(earlier, later):
    return (earlier[0] + later[0], earlier[1] + later[1])


def depthwise(padded, weights, bias, rows, cols):
    total = jnp.zeros((padded.shape[0], rows, cols, padded.shape[3]), jnp.float32) + bias
    for above in range(3):
        for across in range(3):
            total = total + weights[above, across] * padded[
                :, above : above + rows, across : across + cols
            ].astype(jnp.float32)
    return total


def row_adder(flat, piece):
    return jnp.dot(flat, piece, preferred_element_type=jnp.float32)


def local(
    stream,
    queries,
    keys,
    values,
    state_in,
    keysum_in,
    attn_gate,
    ffn_shift,
    ffn_scale,
    w_up,
    conv_weight,
    conv_bias,
):
    frames, rows, cols, width = stream.shape
    heads, head_size = keysum_in.shape
    count = rows * cols
    high = lax.Precision.HIGHEST
    key_feat = jnp.maximum(keys, 0).reshape(frames, count, heads, head_size)
    value_rows = values.reshape(frames, count, heads, head_size)
    query_feat = jnp.maximum(queries.astype(jnp.float32), 0.0).reshape(
        frames, count, heads, head_size
    )
    frame_kv = jnp.einsum(
        "fthd,fthe->fhde", key_feat, value_rows, preferred_element_type=jnp.float32
    )
    frame_keys = jnp.sum(key_feat.astype(jnp.float32), axis=1)
    frame_kv, frame_keys = lax.psum((frame_kv, frame_keys), "space")
    totals = (jnp.sum(frame_kv, axis=0), jnp.sum(frame_keys, axis=0))
    empty = (jnp.zeros_like(totals[0]), jnp.zeros_like(totals[1]))
    prior = entering(totals, "tm", add_totals, empty)
    state = state_in + prior[0] + jnp.cumsum(frame_kv, axis=0)
    keysum = keysum_in + prior[1] + jnp.cumsum(frame_keys, axis=0)
    numerator = jnp.einsum("fthd,fhde->fthe", query_feat, state, precision=high)
    denominator = jnp.einsum("fthd,fhd->fth", query_feat, keysum, precision=high) + 1.0
    attn = (numerator / denominator[..., None]).reshape(frames, rows, cols, width)
    mixed = (stream.astype(jnp.float32) + attn_gate * attn).astype(jnp.bfloat16)
    mixed_f = lax.optimization_barrier(mixed).astype(jnp.float32)
    mean = jnp.mean(mixed_f, axis=-1, keepdims=True)
    centered = mixed_f - mean
    variance = jnp.mean(centered * centered, axis=-1, keepdims=True)
    normed = centered * lax.rsqrt(variance + EPS)
    modulated = (normed * (1.0 + ffn_scale) + ffn_shift).astype(jnp.bfloat16)
    flat = modulated.reshape(frames * count, width)
    up = row_adder(flat, lax.all_gather(w_up, "tm", axis=0, tiled=True))
    up = up.astype(jnp.bfloat16).reshape(frames, rows, cols, w_up.shape[1])
    padded = with_halo(up, (("space", 1),), 1)
    padded = jnp.pad(padded, ((0, 0), (0, 0), (1, 1), (0, 0)))
    conv = depthwise(padded, conv_weight, conv_bias, rows, cols)
    half = conv.shape[3] // 2
    hidden = (conv[..., :half] * jax.nn.silu(conv[..., half:])).astype(jnp.bfloat16)
    return (mixed, hidden)


def solution(mesh):
    placed = (
        P("tm", "space", None, None),
        P("tm", "space", None, None),
        P("tm", "space", None, None),
        P("tm", "space", None, None),
        P(),
        P(),
        P(),
        P(),
        P(),
        P("tm", None),
        P(),
        P(),
    )
    return jax.shard_map(
        local,
        mesh=mesh,
        in_specs=placed,
        out_specs=(P("tm", "space", None, None), P("tm", "space", None, None)),
        check_vma=False,
    )
```

profile of v0, /device:TPU:19, one launch (start us, length us, event | category | flops | bytes accessed | tf_op | source)
XLA Modules:
  0.0 423.8 jit_solution(11415662982019074504)
XLA Ops:
  10.3 5.0 %reshape.51 = bf16[2,240,20,112]{3,2,1,0:T(8,128)(2,1)S(1)} reshape(bf16[2,6,40,2240]{3,2,1,0:T(8,128)(2,1)} %broadcast_maximum_fusion) | data formatting | bytes 4300800 | tf_op jit(solution)/shard_map/reshape | solution.py:79
  15.3 6.2 %reshape.52 = bf16[2,240,20,112]{3,2,1,0:T(8,128)(2,1)} reshape(bf16[2,6,40,2240]{3,2,1,0:T(8,128)(2,1)} %param.17) | data formatting | bytes 4300800 | tf_op jit(solution)/shard_map/reshape | solution.py:80
  21.5 4.2 fusion.13
  25.7 68.2 %all-reduce.3.cloned.1.call-done = f32[2,20,112,112]{3,2,1,0:T(8,128)} async-done(((f32[2,20,112,112]{3,2,1,0:T(8,128)}), f32[2,20,112,112]{3,2,1,0:T(8,128)}) %all-reduce.3.cloned.1.call-update) | async-done | bytes 2007056 | tf_op jit(solution)/shard_map/psum | solution.py:88
  98.3 5.6 %psum.15 = f32[2,20,112]{2,1,0:T(8,128)S(1)} all-reduce(f32[2,20,112]{2,1,0:T(8,128)S(1)} %reduce_sum.49), channel_id=1, replica_groups=mesh['tm'=16,'space'=2] {'space'}, use_global_device_ids=true, to_apply=%region_3.0 | all-reduce | flops 4480 | bytes 35840 | tf_op jit(solution)/shard_map/psum | solution.py:88
  104.0 4.5 %convert_maximum_fusion = f32[2,6,40,2240]{3,2,1,0:T(8,128)} fusion(bf16[2,6,40,2240]{3,2,1,0:T(8,128)(2,1)} %param.15), kind=kLoop, calls=%fused_computation.26 | loop fusion | flops 2150400 | bytes 6451200 | tf_op jit(solution)/shard_map/max | solution.py:81
  108.4 7.2 %reshape.53 = f32[2,240,20,112]{3,2,1,0:T(8,128)} reshape(f32[2,6,40,2240]{3,2,1,0:T(8,128)} %convert_maximum_fusion) | data formatting | bytes 8601600 | tf_op jit(solution)/shard_map/reshape | solution.py:81
  115.6 6.1 %copy.27 = f32[2,240,20,112]{1,3,2,0:T(8,128)} copy(f32[2,240,20,112]{3,2,1,0:T(8,128)} %reshape.53) | data formatting | bytes 8601600 | tf_op jit(solution)/shard_map/reshape | solution.py:81
  121.8 19.7 %all-gather.2 = f32[16,20,112]{2,1,0:T(8,128)} all-gather(f32[1,20,112]{2,1,0:T(8,128)S(1)} %bitcast.41), channel_id=3, replica_groups=mesh['tm'=16,'space'=2] {'tm'}, dimensions={0}, use_global_device_ids=true | all-gather | bytes 152320 | tf_op jit(solution)/shard_map/all_gather | solution.py:11
  143.0 51.9 %all-gather.7.cloned.1.call-done = f32[320,112,112]{2,1,0:T(8,128)} async-done(((f32[20,112,112]{2,1,0:T(8,128)}), f32[320,112,112]{2,1,0:T(8,128)}) %all-gather.7.cloned.1.call-update) | async-done | bytes 16056336 | tf_op jit(solution)/shard_map/all_gather | solution.py:11
  195.0 37.8 %while.16 = (s32[]{:T(128)}, f32[20,112,112]{2,1,0:T(8,128)S(1)}, f32[20,112]{1,0:T(8,128)S(1)}, s32[]{:T(128)}, f32[16,20,112,112]{3,2,1,0:T(8,128)}, /*index=5*/f32[16,20,112]{2,1,0:T(8,128)}, s32[]{:T(128)}, s32[]{:T(128)}) while((s32[]{:T(128)}, f32[20,112,112]{2,1,0:T(8,128)S(1)}, f32[20,112]{1,0:T(8,128)S(1)}, s32[]{:T(128)}, ...), condition=%wide.region_6.7_spmd.clone, body=%wide.region_5.6_spmd.clone.sunk | while | flops 759364 | bytes 3037563 | solution.py:23
  233.0 4.7 %fusion.23 = f32[2,20,1,240]{3,2,1,0:T(1,128)S(1)} fusion(f32[2,240,20,112]{1,3,2,0:T(8,128)} %copy.27, f32[2,20,112,1]{2,1,0,3:T(8,128)S(1)} %fusion.21), kind=kOutput, calls=%fused_computation.48 | convolution fusion | flops 12902400 | bytes 4357120 | tf_op jit(solution)/shard_map/fthd,fhd->fth/dot_general | solution.py:95
  237.7 8.9 %bitcast_divide_fusion = f32[2,240,20,112]{1,3,2,0:T(8,128)} fusion(f32[2,240,20]{1,2,0:T(8,128)S(1)} %fusion.22, f32[2,240,20,112]{1,3,2,0:T(8,128)} %copy.27, f32[2,20,112,112]{3,2,1,0:T(8,128)S(1)} %copy-done.4, f32[20,112,112]{2,1,0:T(8,128)S(1)} %add.137), kind=kOutput, calls=%fused_computation.20 | convolution fusion | flops 1446645760 | bytes 11650560 | tf_op jit(solution)/shard_map/fthd,fhde->fthe/dot_general | solution.py:94
  246.6 6.1 %copy.28 = f32[2,240,20,112]{3,2,1,0:T(8,128)} copy(f32[2,240,20,112]{1,3,2,0:T(8,128)} %bitcast_divide_fusion) | data formatting | bytes 8601600 | tf_op jit(solution)/shard_map/div | solution.py:96
  252.7 7.0 %reshape.54 = f32[2,6,40,2240]{3,2,1,0:T(8,128)} reshape(f32[2,240,20,112]{3,2,1,0:T(8,128)} %copy.28) | data formatting | bytes 8601600 | tf_op jit(solution)/shard_map/reshape | solution.py:96
  259.7 3.6 add_convert_fusion
  266.7 62.9 %all-gather.9.cloned.1.call-done = bf16[16,140,5600]{2,1,0:T(8,128)(2,1)} async-done(((bf16[1,140,5600]{2,1,0:T(8,128)(2,1)}), bf16[16,140,5600]{2,1,0:T(8,128)(2,1)}) %all-gather.9.cloned.1.call-update) | async-done | bytes 25088016 | tf_op jit(solution)/shard_map/all_gather | solution.py:105
  329.5 23.3 %reshape.62 = bf16[2240,5600]{1,0:T(8,128)(2,1)} reshape(bf16[16,140,5600]{2,1,0:T(8,128)(2,1)} %all-gather.9.cloned.1.call-done) | data formatting | bytes 50176000
  352.8 18.2 %convolution_convert_fusion = bf16[480,5600]{1,0:T(8,128)(2,1)S(1)} fusion(bf16[480,2240]{1,0:T(8,128)(2,1)} %bitcast.38, bf16[2240,5600]{1,0:T(8,128)(2,1)} %reshape.62), kind=kOutput, calls=%fused_computation.9 | convolution fusion | flops 12044928000 | bytes 32614400 | tf_op jit(solution)/shard_map/dot_general | solution.py:58
  371.2 3.2 collective-permute-start
  376.2 17.1 %collective-permute-done = bf16[2,1,40,5600]{3,2,1,0:T(8,128)(2,1)S(1)} collective-permute-done((bf16[2,1,40,5600]{3,2,1,0:T(8,128)(2,1)S(1)}, bf16[2,1,40,5600]{3,2,1,0:T(8,128)(2,1)S(1)}, u32[]{:S(2)}, u32[]{:S(2)}) %collective-permute-start) | collective-permute-done | bytes 896032 | tf_op jit(solution)/shard_map/ppermute | solution.py:34
  393.3 3.9 collective-permute-done.1
  397.2 3.3 fusion.5
  400.6 13.8 %multiply_add_fusion = f32[2,6,40,5600]{3,2,1,0:T(8,128)S(1)} fusion(bf16[2,6,40,5600]{3,2,1,0:T(8,128)(2,1)} %bitcast.37, bf16[2,8,42,5600]{3,2,1,0:T(8,128)(2,1)S(1)} %fusion.5, bf16[2,1,40,5600]{3,2,1,0:T(8,128)(2,1)S(1)} %collective-permute-done.1, bf16[2,1,40,5600]{3,2,1,0:T(8,128)(2,1)S(1)} %collective-permute-done, f32[5600]{0:T(1024)S(1)} %get-tuple-element.142, ...), kind=kLoop, calls=%fused_computation.5 | loop fusion | flops 77952000 | bytes 50400000 | tf_op jit(solution)/shard_map/add | solution.py:51
  (84 shorter events, 54.9 us)
Async XLA Ops:
  7.2 86.8 %all-reduce.3.cloned.1.call-start = ((), (), s32[]{:S(2)}) async-start(), calls=%async_computation | async-start | bytes 4587520 | tf_op jit(solution)/shard_map/psum | solution.py:88
  25.7 72.1 %copy-start.3 = (bf16[2,6,40,2240]{3,2,1,0:T(8,128)(2,1)S(1)}, bf16[2,6,40,2240]{3,2,1,0:T(8,128)(2,1)}, u32[]{:S(2)}) copy-start(bf16[2,6,40,2240]{3,2,1,0:T(8,128)(2,1)} %param.16) | copy-start | bytes 6451204
  25.7 169.3 %all-gather.7.cloned.1.call-start = ((), (), s32[]{:S(2)}) async-start(), calls=%async_computation.1 | async-start | bytes 19496960 | tf_op jit(solution)/shard_map/all_gather | solution.py:11
  97.0 232.6 %all-gather.9.cloned.1.call-start = ((), (), s32[]{:S(2)}) async-start(), calls=%async_computation.2 | async-start | bytes 27574272 | tf_op jit(solution)/shard_map/all_gather | solution.py:105
  115.6 25.9 %copy-start.9 = (f32[2240]{0:T(1024)S(1)}, f32[2240]{0:T(1024)}, u32[]{:S(2)}) copy-start(f32[2240]{0:T(1024)} %param.22) | copy-start | bytes 26884
  115.6 25.9 %copy-start.2 = (f32[2,20,112,112]{3,2,1,0:T(8,128)S(1)}, f32[2,20,112,112]{3,2,1,0:T(8,128)}, u32[]{:S(2)}) copy-start(f32[2,20,112,112]{3,2,1,0:T(8,128)} %all-reduce.3.cloned.1.call-done) | copy-start | bytes 6021124
  195.0 37.8 %copy-start.10 = (f32[20,112]{1,0:T(8,128)S(1)}, f32[20,112]{1,0:T(8,128)}, u32[]{:S(2)}) copy-start(f32[20,112]{1,0:T(8,128)} %param.19) | copy-start | bytes 26884
  195.0 37.8 %copy-start.5 = (f32[20,112,112]{2,1,0:T(8,128)S(1)}, f32[20,112,112]{2,1,0:T(8,128)}, u32[]{:S(2)}) copy-start(f32[20,112,112]{2,1,0:T(8,128)} %param.18) | copy-start | bytes 3010564
  232.8 4.9 %copy-start.4 = (f32[2,20,112,112]{3,2,1,0:T(8,128)S(1)}, f32[2,20,112,112]{3,2,1,0:T(8,128)}, u32[]{:S(2)}) copy-start(f32[2,20,112,112]{3,2,1,0:T(8,128)} %fusion.26) | copy-start | bytes 6021124
  252.7 7.0 %copy-start.8 = (f32[2240]{0:T(1024)S(1)}, f32[2240]{0:T(1024)}, u32[]{:S(2)}) copy-start(f32[2240]{0:T(1024)} %param.20) | copy-start | bytes 26884
  259.7 4.7 %copy-start.11 = (f32[2240]{0:T(1024)S(1)}, f32[2240]{0:T(1024)}, u32[]{:S(2)}) copy-start(f32[2240]{0:T(1024)} %param.21) | copy-start | bytes 26884
  263.3 89.5 %copy-start = (bf16[2,6,40,2240]{3,2,1,0:T(8,128)(2,1)}, bf16[2,6,40,2240]{3,2,1,0:T(8,128)(2,1)S(1)}, u32[]{:S(2)}) copy-start(bf16[2,6,40,2240]{3,2,1,0:T(8,128)(2,1)S(1)} %add_convert_fusion) | copy-start | bytes 6451204
  352.8 22.8 %copy-start.6 = (f32[3,3,5600]{2,1,0:T(4,128)S(1)}, f32[3,3,5600]{2,1,0:T(4,128)}, u32[]{:S(2)}) copy-start(f32[3,3,5600]{2,1,0:T(4,128)} %param.24) | copy-start | bytes 604804
  371.0 29.6 %copy-start.1 = (bf16[480,5600]{1,0:T(8,128)(2,1)}, bf16[480,5600]{1,0:T(8,128)(2,1)S(1)}, u32[]{:S(2)}) copy-start(bf16[480,5600]{1,0:T(8,128)(2,1)S(1)} %convolution_convert_fusion) | copy-start | bytes 16128004
  371.2 22.2 %collective-permute-start = (bf16[2,1,40,5600]{3,2,1,0:T(8,128)(2,1)S(1)}, bf16[2,1,40,5600]{3,2,1,0:T(8,128)(2,1)S(1)}, u32[]{:S(2)}, u32[]{:S(2)}) collective-permute-start(bf16[2,1,40,5600]{3,2,1,0:T(8,128)(2,1)S(1)} %get-tuple-element.156), channel_id=1, source_target_pairs={{0,1},{2,3},{4,5},{6,7},{8,9},{10,11},{12,13},{14,15},{16,17},{18,... | collective-permute-start | bytes 2688008 | tf_op jit(solution)/shard_map/ppermute | solution.py:34
  374.3 22.9 %collective-permute-start.1 = (bf16[2,1,40,5600]{3,2,1,0:T(8,128)(2,1)S(1)}, bf16[2,1,40,5600]{3,2,1,0:T(8,128)(2,1)S(1)}, u32[]{:S(2)}, u32[]{:S(2)}) collective-permute-start(bf16[2,1,40,5600]{3,2,1,0:T(8,128)(2,1)S(1)} %get-tuple-element.157), channel_id=1, source_target_pairs={{1,0},{3,2},{5,4},{7,6},{9,8},{11,10},{13,12},{15,14},{17,16},{19,... | collective-permute-start | bytes 2688008 | tf_op jit(solution)/shard_map/ppermute | solution.py:36
  376.2 24.4 %copy-start.7 = (f32[5600]{0:T(1024)S(1)}, f32[5600]{0:T(1024)}, u32[]{:S(2)}) copy-start(f32[5600]{0:T(1024)} %param.25) | copy-start | bytes 67204
Sparse Core Ops, SparseCore 0:
  25.8 68.1 all-reduce.2
  97.1 97.8 all-gather.6
  196.6 132.9 all-gather.8
where the time goes:
time: 429 us; the launch traced here: 424 us
  waiting for transfers between devices  205 us (48%)
  other arithmetic  77.1 us (18%)
  local copies, waits for them, and re-layouts  61.6 us (14%)
  matrix products  36 us (8%)
  blocking collectives  25.4 us (6%)
  between operations  14 us (3%)
  starting transfers between devices  4.57 us (1%)
    psum x1, waiting for transfers between devices, local(): frame_kv, frame_keys = lax.psum((frame_kv, frame_keys), 'space')  68.2 us
    all_gather x1, waiting for transfers between devices, local(): up = row_adder(flat, lax.all_gather(w_up, 'tm', axis=0, tiled=True))  62.9 us
    all_gather x1, waiting for transfers between devices, entering(): everything = jax.tree.map(lambda part: lax.all_gather(part, axis), array)  51.9 us
    select_n x32, other arithmetic, step(): return jax.tree.map(lambda a, b: jnp.where(reached, a, b), new, before)  37.4 us
    unnamed x25, local copies, waits for them, and re-layouts  23.3 us
    all_gather x1, blocking collectives, entering(): everything = jax.tree.map(lambda part: lax.all_gather(part, axis), array)  19.7 us
    dot_general x1, matrix products, row_adder(): return jnp.dot(flat, piece, preferred_element_type=jnp.float32)  18.2 us
    ppermute x1, waiting for transfers between devices, with_halo(): lax.ppermute(tail, axis, [(i, (i + 1) % count) for i in range(ends)])  17.1 us
  transfers between devices with their start and end apart: 5, of which 5 were waited for; matrix products, arithmetic and copies ran while one was open for 22% of the time, Pallas kernels for 0%

commit v1 on v0

v1 whole, which is shorter than its diff:
```python
import functools

import jax
import jax.numpy as jnp
from jax import lax
from jax.experimental import pallas as pl
from jax.experimental.pallas import tpu as pltpu
from jax.sharding import PartitionSpec as P

EPS = 1e-06
LANES = 128
BF16 = jnp.bfloat16
F32 = jnp.float32
PARAMS = pltpu.CompilerParams(
    dimension_semantics=("arbitrary",), vmem_limit_bytes=56 * 1024 * 1024
)


def up_to(size, step):
    return -(-size // step) * step


def kv_kernel(heads, head_size, parts, place, k_ref, v_ref, *refs):
    outs, held = refs[:parts], refs[parts]
    tokens = k_ref.shape[1]
    each = heads // parts
    feats = jnp.maximum(k_ref[0], 0)
    vals = v_ref[0]
    ones = jnp.ones((tokens, LANES - head_size), BF16)
    for h in range(heads):
        lanes = slice(h * head_size, (h + 1) * head_size)
        right = jnp.concatenate([vals[:, lanes], ones], axis=1)
        held[h] = lax.dot_general(
            feats[:, lanes],
            right,
            (((0,), (0,)), ((), ())),
            preferred_element_type=F32,
        ).astype(BF16)
    for part in range(parts):
        slot = lax.rem(part - place[0] + parts, parts)
        for k in range(parts):

            @pl.when(slot == k)
            def _():
                outs[k][0] = held[part * each : (part + 1) * each]


def attn_kernel(
    heads, head_size, parts, deep, deep_pad, cols, place, q_ref, s_ref, in_ref, gate, shift, scale, *refs
):
    gathered = refs[:parts]
    mixed_ref, x_ref = refs[parts], refs[parts + 1]
    edges = refs[parts + 2 : -1]
    attn = refs[-1]
    tokens, width = q_ref.shape[1:]
    each = heads // parts
    feats = jnp.maximum(q_ref[0], 0)
    for h in range(heads):
        part, i = divmod(h, each)
        slot = lax.rem(place[0] - part + parts, parts)
        state = gathered[0][0, i].astype(F32)
        for k in range(1, parts):
            state = jnp.where(slot == k, gathered[k][0, i].astype(F32), state)
        state = state + in_ref[h]
        high = state.astype(BF16)
        low = (state - high.astype(F32)).astype(BF16)
        lanes = slice(h * head_size, (h + 1) * head_size)
        both = jnp.dot(
            feats[:, lanes], jnp.concatenate([high, low], axis=1), preferred_element_type=F32
        )
        sums = both[:, :LANES] + both[:, LANES:]
        below = sums[:, head_size : head_size + 1] + 1.0
        attn[:, lanes] = sums[:, :head_size] * (1.0 / below)
    mixed = (s_ref[0].astype(F32) + gate[...] * attn[...]).astype(BF16)
    mixed_ref[0] = mixed
    wide = mixed.astype(F32)
    mean = jnp.sum(wide, axis=1, keepdims=True) * (1.0 / width)
    centered = wide - mean
    variance = jnp.sum(centered * centered, axis=1, keepdims=True) * (1.0 / width)
    normed = centered * lax.rsqrt(variance + EPS)
    modulated = (normed * (1.0 + scale[...]) + shift[...]).astype(BF16)
    blank = jnp.zeros((tokens, deep_pad - deep), BF16)
    pieces = []
    for t in range(width // deep):
        pieces += [modulated[:, t * deep : (t + 1) * deep], blank]
    rows = jnp.concatenate(pieces, axis=1)
    x_ref[0] = rows
    if len(edges) == 1:
        edges[0][0] = jnp.where(place[0] == 0, rows[tokens - cols :], rows[:cols])
    else:
        edges[0][0] = rows[:cols]
        edges[1][0] = rows[tokens - cols :]


def ffn_kernel(frames, rows, cols, halos, place, x_ref, *refs):
    halo = refs[:halos]
    wv, wg, cv, cg, bv, bg, out, xs, left, mid, right = refs[halos:]
    own = frames * rows * cols
    edge = frames * cols

    @pl.when(pl.program_id(0) == 0)
    def _():
        xs[:own] = x_ref[...]
        for k in range(halos):
            xs[own + k * edge : own + (k + 1) * edge] = halo[k][...]

    total = own + halos * edge
    at = lax.rem(lax.broadcasted_iota(jnp.int32, (total, 1), 0), cols)
    first, last = at == 0, at == cols - 1
    above_ok = place[0] > 0
    for side, (w, c, b) in enumerate(((wv, cv, bv), (wg, cg, bg))):
        up = jnp.dot(xs[...], w[...], preferred_element_type=F32).astype(BF16).astype(F32)
        mid[side] = up
        left[side] = jnp.where(first, 0.0, pltpu.roll(up, 1, 0))
        right[side] = jnp.where(last, 0.0, pltpu.roll(up, total - 1, 0))

    def row_of(side, f, r):
        if 0 <= r < rows:
            at = slice((f * rows + r) * cols, (f * rows + r + 1) * cols)
            return [ref[side, at] for ref in (left, mid, right)]
        if halos == 1:
            at = slice(own + f * cols, own + (f + 1) * cols)
            used = above_ok if r < 0 else jnp.logical_not(above_ok)
            return [jnp.where(used, ref[side, at], 0.0) for ref in (left, mid, right)]
        start = own + (0 if r < 0 else edge) + f * cols
        at = slice(start, start + cols)
        return [ref[side, at] for ref in (left, mid, right)]

    for f in range(frames):
        for r in range(rows):
            convs = []
            for side, (c, b) in enumerate(((cv, bv), (cg, bg))):
                total_row = jnp.broadcast_to(b[...], (cols, b.shape[1]))
                for above in range(3):
                    three = row_of(side, f, r + above - 1)
                    for across in range(3):
                        k = above * 3 + across
                        total_row = total_row + c[k : k + 1] * three[across]
                convs.append(total_row)
            value, gate = convs
            at = slice((f * rows + r) * cols, (f * rows + r + 1) * cols)
            out[at] = (value * (gate * (1.0 / (1.0 + jnp.exp(-gate))))).astype(BF16)


def local(
    stream,
    queries,
    keys,
    values,
    state_in,
    keysum_in,
    attn_gate,
    ffn_shift,
    ffn_scale,
    w_up,
    conv_weight,
    conv_bias,
):
    frames, rows, cols, width = stream.shape
    heads, head_size = keysum_in.shape
    tokens = rows * cols
    parts = lax.axis_size("space")
    peers = lax.axis_size("tm")
    each = heads // parts
    half = w_up.shape[1] // 2
    block = 2 * LANES
    half_pad = up_to(half, block)
    deep = w_up.shape[0]
    deep_pad = up_to(deep, 8)
    depth = peers * deep_pad
    place = lax.axis_index("space").astype(jnp.int32).reshape(1)

    def round_space(array, k):
        return lax.ppermute(array, "space", [(i, (i + k) % parts) for i in range(parts)])

    def filled(array):
        side = jnp.zeros(array.shape[:-1] + (half_pad - half,), array.dtype)
        return jnp.concatenate([array[..., :half], side, array[..., half:], side], axis=-1)

    weights = jnp.pad(filled(w_up), ((0, deep_pad - deep), (0, 0)))
    weights = lax.all_gather(weights, "tm", axis=0).reshape(depth, 2 * half_pad)
    taps = filled(conv_weight.reshape(9, 2 * half))
    bias = filled(conv_bias.reshape(1, 2 * half))

    def frame_block(*shape):
        return pl.BlockSpec((1,) + shape, lambda f, _: (f,) + (0,) * len(shape))

    def whole(*shape):
        return pl.BlockSpec(shape, lambda f, _: (0,) * len(shape))

    flat = (frames, tokens, width)
    part_shape = (each, head_size, LANES)
    sums = pl.pallas_call(
        functools.partial(kv_kernel, heads, head_size, parts),
        grid_spec=pltpu.PrefetchScalarGridSpec(
            num_scalar_prefetch=1,
            grid=(frames,),
            in_specs=[frame_block(tokens, width)] * 2,
            out_specs=[frame_block(*part_shape)] * parts,
            scratch_shapes=[pltpu.VMEM((heads, head_size, LANES), BF16)],
        ),
        out_shape=[jax.ShapeDtypeStruct((frames,) + part_shape, BF16)] * parts,
        compiler_params=PARAMS,
        name="frame_sums",
    )(place, keys.reshape(flat), values.reshape(flat))
    mine = sums[0].astype(F32)
    for k in range(1, parts):
        mine = mine + round_space(sums[k], k).astype(F32)
    running = jnp.sum(mine, axis=0)
    prior = jnp.zeros_like(running)
    step = 1
    while step < peers:
        got = lax.ppermute(
            running.astype(BF16), "tm", [(i, i + step) for i in range(peers - step)]
        ).astype(F32)
        prior = prior + got
        running = running + got
        step *= 2
    states = (prior + jnp.cumsum(mine, axis=0)).astype(BF16)
    gathered = [states] + [round_space(states, k) for k in range(1, parts)]
    start = jnp.concatenate(
        [state_in, jnp.broadcast_to(keysum_in[..., None], (heads, head_size, LANES - head_size))],
        axis=-1,
    )
    halos = 1 if parts == 2 else 2
    mixed, x, *edges = pl.pallas_call(
        functools.partial(attn_kernel, heads, head_size, parts, deep, deep_pad, cols),
        grid_spec=pltpu.PrefetchScalarGridSpec(
            num_scalar_prefetch=1,
            grid=(frames,),
            in_specs=[frame_block(tokens, width)] * 2
            + [whole(heads, head_size, LANES)]
            + [whole(1, width)] * 3
            + [frame_block(*part_shape)] * parts,
            out_specs=[frame_block(tokens, width), frame_block(tokens, depth)]
            + [frame_block(cols, depth)] * halos,
            scratch_shapes=[pltpu.VMEM((tokens, width), F32)],
        ),
        out_shape=[
            jax.ShapeDtypeStruct(flat, BF16),
            jax.ShapeDtypeStruct((frames, tokens, depth), BF16),
        ]
        + [jax.ShapeDtypeStruct((frames, cols, depth), BF16)] * halos,
        compiler_params=PARAMS,
        name="attention",
    )(
        place,
        queries.reshape(flat),
        stream.reshape(flat),
        start,
        attn_gate.reshape(1, width),
        ffn_shift.reshape(1, width),
        ffn_scale.reshape(1, width),
        *gathered,
    )
    if halos == 1:
        around = [round_space(edges[0], 1)]
    else:
        around = [
            lax.ppermute(edges[1], "space", [(i, i + 1) for i in range(parts - 1)]),
            lax.ppermute(edges[0], "space", [(i + 1, i) for i in range(parts - 1)]),
        ]
    blocks = half_pad // block
    own = frames * tokens
    total = own + halos * frames * cols

    def column(height, shift):
        return pl.BlockSpec((height, block), lambda j, _: (0, j + shift))

    hidden = pl.pallas_call(
        functools.partial(ffn_kernel, frames, rows, cols, halos),
        grid_spec=pltpu.PrefetchScalarGridSpec(
            num_scalar_prefetch=1,
            grid=(blocks,),
            in_specs=[whole(own, depth)]
            + [whole(frames * cols, depth)] * halos
            + [column(depth, 0), column(depth, blocks)]
            + [column(9, 0), column(9, blocks), column(1, 0), column(1, blocks)],
            out_specs=column(own, 0),
            scratch_shapes=[pltpu.VMEM((total, depth), BF16)]
            + [pltpu.VMEM((2, total, block), F32)] * 3,
        ),
        out_shape=jax.ShapeDtypeStruct((own, half), BF16),
        compiler_params=PARAMS,
        name="mix_ffn",
    )(
        place,
        x.reshape(own, depth),
        *[a.reshape(frames * cols, depth) for a in around],
        weights,
        weights,
        taps,
        taps,
        bias,
        bias,
    )
    return mixed.reshape(stream.shape), hidden.reshape(frames, rows, cols, half)


def solution(mesh):
    placed = (
        P("tm", "space", None, None),
        P("tm", "space", None, None),
        P("tm", "space", None, None),
        P("tm", "space", None, None),
        P(),
        P(),
        P(),
        P(),
        P(),
        P("tm", None),
        P(),
        P(),
    )
    return jax.shard_map(
        local,
        mesh=mesh,
        in_specs=placed,
        out_specs=(P("tm", "space", None, None), P("tm", "space", None, None)),
        check_vma=False,
    )
```

time: 429 us -> 211 us (0.49); the launches traced: 424 us -> 210 us
  waiting for transfers between devices: 205 us -> 113 us
  other arithmetic: 77.1 us -> 3.38 us
  Pallas kernels: 0 us -> 54.9 us
  local copies, waits for them, and re-layouts: 61.6 us -> 8.82 us
  matrix products: 36 us -> 0 us
  blocking collectives: 25.4 us -> 0 us
  starting transfers between devices: 4.57 us -> 16.1 us
    all_gather x2 -> x1, waiting for transfers between devices: 115 us -> 40.7 us  [local(): weights = lax.all_gather(weights, 'tm', axis=0).reshape(depth, 2 * half_pad)]
    psum x1 -> x0, waiting for transfers between devices: 68.2 us -> none  [local(): frame_kv, frame_keys = lax.psum((frame_kv, frame_keys), 'space')]
    pallas_call x0 -> x3, Pallas kernels: none -> 54.9 us  [the longest x1 31.7 us: local(): pl.pallas_call(functools.partial(ffn_kernel, frames, rows, cols, halos),...]
    ppermute x2 -> x7, waiting for transfers between devices: 21 us -> 72.2 us  [the longest x4 48 us: local(): lax.ppermute(running.astype(BF16), 'tm', [(i, i + step) for i in range(pe...]
    select_n x32 -> x0, other arithmetic: 37.4 us -> none  [step(): return jax.tree.map(lambda a, b: jnp.where(reached, a, b), new, before)]
    dot_general x4 -> x0, matrix products: 36 us -> none  [the longest x1 18.2 us: row_adder(): return jnp.dot(flat, piece, preferred_element_type=jnp.float32)]
    reshape x5, local copies, waits for them, and re-layouts: 31.4 us -> 1.93 us  [the longest x1 0.61 us: local(): ffn_scale.reshape(1, width)]
    unnamed x25 -> x22, local copies, waits for them, and re-layouts: 23.3 us -> 0.87 us
  transfers between devices with their start and end apart: 5 -> 8, of which waited for: 5 -> 8; matrix products, arithmetic and copies ran while one was open for 22% -> 3% of each run, Pallas kernels for 0% -> 11%
where the time goes in v1:
time: 211 us; the launch traced here: 210 us
  waiting for transfers between devices  113 us (54%)
  Pallas kernels  54.9 us (26%)
  starting transfers between devices  16.1 us (8%)
  between operations  14.3 us (7%)
  local copies, waits for them, and re-layouts  8.82 us (4%)
  other arithmetic  3.38 us (2%)
    ppermute x4, waiting for transfers between devices, local(): lax.ppermute(running.astype(BF16), 'tm', [(i, i + step) for i in range(pe...  48 us
    all_gather x1, waiting for transfers between devices, local(): weights = lax.all_gather(weights, 'tm', axis=0).reshape(depth, 2 * half_pad)  40.7 us
    pallas_call x1, Pallas kernels, local(): pl.pallas_call(functools.partial(ffn_kernel, frames, rows, cols, halos),...  31.7 us
    ppermute x3, waiting for transfers between devices, round_space(): lax.ppermute(array, 'space', [(i, (i + k) % parts) for i in range(parts)])  24.1 us
    pallas_call x1, Pallas kernels, local(): pl.pallas_call(functools.partial(attn_kernel, heads, head_size, parts, de...  16 us
    ppermute x4, starting transfers between devices, local(): lax.ppermute(running.astype(BF16), 'tm', [(i, i + step) for i in range(pe...  12.2 us
    pallas_call x1, Pallas kernels, local(): pl.pallas_call(functools.partial(kv_kernel, heads, head_size, parts), gri...  7.26 us
  transfers between devices with their start and end apart: 8, of which 8 were waited for; matrix products, arithmetic and copies ran while one was open for 3% of the time, Pallas kernels for 11%

profile of v1, /device:TPU:19, one launch (start us, length us, event | category | flops | bytes accessed | tf_op | source)
XLA Modules:
  0.0 210.4 jit_solution(9128743912770033356)
XLA Ops:
  7.2 1.7 fusion.6
  8.9 1.0 concatenate.13
  10.0 1.3 pad.4
  11.2 7.3 %frame_sums.1 = (bf16[2,10,112,128]{3,2,1,0:T(8,128)(2,1)}, bf16[2,10,112,128]{3,2,1,0:T(8,128)(2,1)}) custom-call(s32[1]{0:T(128)} %bitcast.place, bf16[2,240,2240]{2,1,0:T(8,128)(2,1)} %bitcast.11, bf16[2,240,2240]{2,1,0:T(8,128)(2,1)} %bitcast.12), custom_call_target="tpu_custom_call" | custom-call | tf_op jit(solution)/shard_map/frame_sums/pallas_call | solution.py:193
  18.5 1.3 collective-permute-start
  19.8 12.9 %collective-permute-done = bf16[2,10,112,128]{3,2,1,0:T(8,128)(2,1)S(1)} collective-permute-done((bf16[2,10,112,128]{3,2,1,0:T(8,128)(2,1)}, bf16[2,10,112,128]{3,2,1,0:T(8,128)(2,1)S(1)}, u32[]{:S(2)}, u32[]{:S(2)}) %collective-permute-start) | collective-permute-done | bytes 573472 | tf_op jit(solution)/shard_map/ppermute | solution.py:174
  32.7 1.3 fusion.1
  34.0 4.5 %collective-permute-start.1 = (bf16[10,112,128]{2,1,0:T(8,128)(2,1)S(1)}, bf16[10,112,128]{2,1,0:T(8,128)(2,1)S(1)}, u32[]{:S(2)}, u32[]{:S(2)}) collective-permute-start(bf16[10,112,128]{2,1,0:T(8,128)(2,1)S(1)} %convert_element_type.37), channel_id=1, source_target_pairs={{0,2},{2,4},{4,6},{6,8},{8,10},{10,12},{12,14},{14,16},{16,18},{18... | collective-permute-start | bytes 860168 | tf_op jit(solution)/shard_map/ppermute | solution.py:213
  38.5 9.8 %collective-permute-done.1 = bf16[10,112,128]{2,1,0:T(8,128)(2,1)S(1)} collective-permute-done((bf16[10,112,128]{2,1,0:T(8,128)(2,1)S(1)}, bf16[10,112,128]{2,1,0:T(8,128)(2,1)S(1)}, u32[]{:S(2)}, u32[]{:S(2)}) %collective-permute-start.1) | collective-permute-done | bytes 286752 | tf_op jit(solution)/shard_map/ppermute | solution.py:213
  48.4 3.1 %collective-permute-start.2 = (bf16[10,112,128]{2,1,0:T(8,128)(2,1)S(1)}, bf16[10,112,128]{2,1,0:T(8,128)(2,1)S(1)}, u32[]{:S(2)}, u32[]{:S(2)}) collective-permute-start(bf16[10,112,128]{2,1,0:T(8,128)(2,1)S(1)} %fusion.4), channel_id=1, source_target_pairs={{0,4},{2,6},{4,8},{6,10},{8,12},{10,14},{12,16},{14,18},{16,20},{1... | collective-permute-start | bytes 860168 | tf_op jit(solution)/shard_map/ppermute | solution.py:213
  51.5 12.0 %collective-permute-done.2 = bf16[10,112,128]{2,1,0:T(8,128)(2,1)S(1)} collective-permute-done((bf16[10,112,128]{2,1,0:T(8,128)(2,1)S(1)}, bf16[10,112,128]{2,1,0:T(8,128)(2,1)S(1)}, u32[]{:S(2)}, u32[]{:S(2)}) %collective-permute-start.2) | collective-permute-done | bytes 286752 | tf_op jit(solution)/shard_map/ppermute | solution.py:213
  63.7 3.1 %collective-permute-start.3 = (bf16[10,112,128]{2,1,0:T(8,128)(2,1)S(1)}, bf16[10,112,128]{2,1,0:T(8,128)(2,1)S(1)}, u32[]{:S(2)}, u32[]{:S(2)}) collective-permute-start(bf16[10,112,128]{2,1,0:T(8,128)(2,1)S(1)} %fusion.5), channel_id=1, source_target_pairs={{0,8},{2,10},{4,12},{6,14},{8,16},{10,18},{12,20},{14,22},{16,24},... | collective-permute-start | bytes 860168 | tf_op jit(solution)/shard_map/ppermute | solution.py:213
  66.8 13.1 %collective-permute-done.3 = bf16[10,112,128]{2,1,0:T(8,128)(2,1)S(1)} collective-permute-done((bf16[10,112,128]{2,1,0:T(8,128)(2,1)S(1)}, bf16[10,112,128]{2,1,0:T(8,128)(2,1)S(1)}, u32[]{:S(2)}, u32[]{:S(2)}) %collective-permute-start.3) | collective-permute-done | bytes 286752 | tf_op jit(solution)/shard_map/ppermute | solution.py:213
  80.0 1.5 collective-permute-start.4
  83.5 13.1 %collective-permute-done.4 = bf16[10,112,128]{2,1,0:T(8,128)(2,1)S(1)} collective-permute-done((bf16[10,112,128]{2,1,0:T(8,128)(2,1)S(1)}, bf16[10,112,128]{2,1,0:T(8,128)(2,1)S(1)}, u32[]{:S(2)}, u32[]{:S(2)}) %collective-permute-start.4) | collective-permute-done | bytes 286752 | tf_op jit(solution)/shard_map/ppermute | solution.py:213
  97.0 1.3 collective-permute-start.5
  99.5 1.4 pad_maximum_fusion.in_ref
  100.9 6.4 %collective-permute-done.5.refs_1_ = bf16[2,10,112,128]{3,2,1,0:T(8,128)(2,1)S(1)} collective-permute-done((bf16[2,10,112,128]{3,2,1,0:T(8,128)(2,1)S(1)}, bf16[2,10,112,128]{3,2,1,0:T(8,128)(2,1)S(1)}, u32[]{:S(2)}, u32[]{:S(2)}) %collective-permute-start.5) | collective-permute-done | bytes 573472 | tf_op jit(solution)/shard_map/ppermute | solution.py:174
  107.3 0.8 copy-done.3
  108.2 16.0 %attention.1 = (bf16[2,240,2240]{2,1,0:T(8,128)(2,1)}, bf16[2,240,2304]{2,1,0:T(8,128)(2,1)}, bf16[2,40,2304]{2,1,0:T(8,128)(2,1)}) custom-call(s32[1]{0:T(128)} %bitcast.place, bf16[2,240,2240]{2,1,0:T(8,128)(2,1)} %bitcast.13, bf16[2,240,2240]{2,1,0:T(8,128)(2,1)} %bitcast.14, f32[20,112,128]{2,1,0:T(8,128)} %pad_maximum_fusion.in_ref, ...), custom_call_target="tpu_custom_call" | custom-call | tf_op jit(solution)/shard_map/attention/pallas_call | solution.py:226
  124.1 1.3 collective-permute-start.6
  126.3 4.8 %collective-permute-done.6 = bf16[2,40,2304]{2,1,0:T(8,128)(2,1)S(1)} collective-permute-done((bf16[2,40,2304]{2,1,0:T(8,128)(2,1)}, bf16[2,40,2304]{2,1,0:T(8,128)(2,1)S(1)}, u32[]{:S(2)}, u32[]{:S(2)}) %collective-permute-start.6) | collective-permute-done | bytes 368672 | tf_op jit(solution)/shard_map/ppermute | solution.py:174
  131.1 40.7 %all-gather.3.cloned.1.call-done.refs_1_.refs_2_ = bf16[2304,5632]{1,0:T(8,128)(2,1)} async-done(((bf16[144,5632]{1,0:T(8,128)(2,1)}), bf16[2304,5632]{1,0:T(8,128)(2,1)}) %all-gather.3.cloned.1.call-update) | async-done | bytes 25952272 | tf_op jit(solution)/shard_map/all_gather | solution.py:181
  171.8 31.7 %mix_ffn.1 = bf16[480,2800]{1,0:T(8,128)(2,1)} custom-call(s32[1]{0:T(128)} %bitcast.place, bf16[480,2304]{1,0:T(8,128)(2,1)} %bitcast.10, bf16[80,2304]{1,0:T(8,128)(2,1)} %bitcast.15, bf16[2304,5632]{1,0:T(8,128)(2,1)} %all-gather.3.cloned.1.call-done.refs_1_.refs_2_, bf16[2304,5632]{1,0:T(8,128)(2,1)} %all-gather.3.cloned.1.call-done.refs_1_.refs_2_, ...), custom_call_target="tpu_custom_call" | custom-call | tf_op jit(solution)/shard_map/mix_ffn/pallas_call | solution.py:270
  (42 shorter events, 4.8 us)
Async XLA Ops:
  7.2 164.6 %all-gather.3.cloned.1.call-start = ((), (), s32[]{:S(2)}) async-start(), calls=%async_computation | async-start | bytes 27574272 | tf_op jit(solution)/shard_map/all_gather | solution.py:181
  18.5 14.2 %collective-permute-start = (bf16[2,10,112,128]{3,2,1,0:T(8,128)(2,1)}, bf16[2,10,112,128]{3,2,1,0:T(8,128)(2,1)S(1)}, u32[]{:S(2)}, u32[]{:S(2)}) collective-permute-start(bf16[2,10,112,128]{3,2,1,0:T(8,128)(2,1)} %get-tuple-element.8), channel_id=1, source_target_pairs={{0,1},{1,0},{2,3},{3,2},{4,5},{5,4},{6,7},{7,6},{8,9},{9,8},{10,11... | collective-permute-start | bytes 1720328 | tf_op jit(solution)/shard_map/ppermute | solution.py:174
  34.0 14.3 %collective-permute-start.1 = (bf16[10,112,128]{2,1,0:T(8,128)(2,1)S(1)}, bf16[10,112,128]{2,1,0:T(8,128)(2,1)S(1)}, u32[]{:S(2)}, u32[]{:S(2)}) collective-permute-start(bf16[10,112,128]{2,1,0:T(8,128)(2,1)S(1)} %convert_element_type.37), channel_id=1, source_target_pairs={{0,2},{2,4},{4,6},{6,8},{8,10},{10,12},{12,14},{14,16},{16,18},{18... | collective-permute-start | bytes 860168 | tf_op jit(solution)/shard_map/ppermute | solution.py:213
  48.4 15.1 %collective-permute-start.2 = (bf16[10,112,128]{2,1,0:T(8,128)(2,1)S(1)}, bf16[10,112,128]{2,1,0:T(8,128)(2,1)S(1)}, u32[]{:S(2)}, u32[]{:S(2)}) collective-permute-start(bf16[10,112,128]{2,1,0:T(8,128)(2,1)S(1)} %fusion.4), channel_id=1, source_target_pairs={{0,4},{2,6},{4,8},{6,10},{8,12},{10,14},{12,16},{14,18},{16,20},{1... | collective-permute-start | bytes 860168 | tf_op jit(solution)/shard_map/ppermute | solution.py:213
  63.7 17.8 %copy-start.8 = (f32[2240]{0:T(1024)S(1)}, f32[2240]{0:T(1024)}, u32[]{:S(2)}) copy-start(f32[2240]{0:T(1024)} %param.18) | copy-start | bytes 26884
  63.7 18.4 %copy-start.9 = (f32[2240]{0:T(1024)S(1)}, f32[2240]{0:T(1024)}, u32[]{:S(2)}) copy-start(f32[2240]{0:T(1024)} %param.19) | copy-start | bytes 26884
  63.7 19.0 %copy-start.10 = (f32[2240]{0:T(1024)S(1)}, f32[2240]{0:T(1024)}, u32[]{:S(2)}) copy-start(f32[2240]{0:T(1024)} %param.20) | copy-start | bytes 26884
  63.7 19.6 %copy-start.6 = (f32[5600]{0:T(1024)S(1)}, f32[5600]{0:T(1024)}, u32[]{:S(2)}) copy-start(f32[5600]{0:T(1024)} %param.23) | copy-start | bytes 67204
  63.7 19.6 %copy-start.5 = (f32[3,3,5600]{2,1,0:T(4,128)S(1)}, f32[3,3,5600]{2,1,0:T(4,128)}, u32[]{:S(2)}) copy-start(f32[3,3,5600]{2,1,0:T(4,128)} %param.22) | copy-start | bytes 604804
  63.7 16.1 %collective-permute-start.3 = (bf16[10,112,128]{2,1,0:T(8,128)(2,1)S(1)}, bf16[10,112,128]{2,1,0:T(8,128)(2,1)S(1)}, u32[]{:S(2)}, u32[]{:S(2)}) collective-permute-start(bf16[10,112,128]{2,1,0:T(8,128)(2,1)S(1)} %fusion.5), channel_id=1, source_target_pairs={{0,8},{2,10},{4,12},{6,14},{8,16},{10,18},{12,20},{14,22},{16,24},... | collective-permute-start | bytes 860168 | tf_op jit(solution)/shard_map/ppermute | solution.py:213
  80.0 16.6 %collective-permute-start.4 = (bf16[10,112,128]{2,1,0:T(8,128)(2,1)S(1)}, bf16[10,112,128]{2,1,0:T(8,128)(2,1)S(1)}, u32[]{:S(2)}, u32[]{:S(2)}) collective-permute-start(bf16[10,112,128]{2,1,0:T(8,128)(2,1)S(1)} %fusion.3), channel_id=1, source_target_pairs={{0,16},{2,18},{4,20},{6,22},{8,24},{10,26},{12,28},{14,30},{1,17},... | collective-permute-start | bytes 860168 | tf_op jit(solution)/shard_map/ppermute | solution.py:213
  83.3 13.4 %copy-start = (bf16[2,10,112,128]{3,2,1,0:T(8,128)(2,1)S(1)}, bf16[2,10,112,128]{3,2,1,0:T(8,128)(2,1)}, u32[]{:S(2)}) copy-start(bf16[2,10,112,128]{3,2,1,0:T(8,128)(2,1)} %get-tuple-element.7) | copy-start | bytes 1720324
  96.7 2.4 %copy-start.7 = (f32[20,112]{1,0:T(8,128)S(1)}, f32[20,112]{1,0:T(8,128)}, u32[]{:S(2)}) copy-start(f32[20,112]{1,0:T(8,128)} %param.17) | copy-start | bytes 26884
  97.0 3.9 %copy-start.1 = (bf16[2,10,112,128]{3,2,1,0:T(8,128)(2,1)}, bf16[2,10,112,128]{3,2,1,0:T(8,128)(2,1)S(1)}, u32[]{:S(2)}) copy-start(bf16[2,10,112,128]{3,2,1,0:T(8,128)(2,1)S(1)} %add_convert_fusion.refs_0_) | copy-start | bytes 1720324
  97.0 2.5 %copy-start.2 = (f32[20,112,112]{2,1,0:T(8,128)S(1)}, f32[20,112,112]{2,1,0:T(8,128)}, u32[]{:S(2)}) copy-start(f32[20,112,112]{2,1,0:T(8,128)} %param.16) | copy-start | bytes 3010564
  97.0 10.3 %collective-permute-start.5 = (bf16[2,10,112,128]{3,2,1,0:T(8,128)(2,1)S(1)}, bf16[2,10,112,128]{3,2,1,0:T(8,128)(2,1)S(1)}, u32[]{:S(2)}, u32[]{:S(2)}) collective-permute-start(bf16[2,10,112,128]{3,2,1,0:T(8,128)(2,1)S(1)} %add_convert_fusion.refs_0_), channel_id=1, source_target_pairs={{0,1},{1,0},{2,3},{3,2},{4,5},{5,4},{6,7},{7,6},{8,9},{9,8},{10,11... | collective-permute-start | bytes 1720328 | tf_op jit(solution)/shard_map/ppermute | solution.py:174
  107.3 0.8 copy-start.3
  124.1 7.0 %collective-permute-start.6 = (bf16[2,40,2304]{2,1,0:T(8,128)(2,1)}, bf16[2,40,2304]{2,1,0:T(8,128)(2,1)S(1)}, u32[]{:S(2)}, u32[]{:S(2)}) collective-permute-start(bf16[2,40,2304]{2,1,0:T(8,128)(2,1)} %get-tuple-element.11), channel_id=1, source_target_pairs={{0,1},{1,0},{2,3},{3,2},{4,5},{5,4},{6,7},{7,6},{8,9},{9,8},{10,11... | collective-permute-start | bytes 1105928 | tf_op jit(solution)/shard_map/ppermute | solution.py:174
  131.1 40.7 %copy-start.4 = (bf16[2,40,2304]{2,1,0:T(8,128)(2,1)}, bf16[2,40,2304]{2,1,0:T(8,128)(2,1)S(1)}, u32[]{:S(2)}) copy-start(bf16[2,40,2304]{2,1,0:T(8,128)(2,1)S(1)} %collective-permute-done.6) | copy-start | bytes 1105924
Sparse Core Ops, SparseCore 0:
  11.4 160.3 all-gather.2

commit v2 on v1

--- a/solution.py
+++ b/solution.py
@@ -9,6 +9,7 @@
 
 EPS = 1e-06
 LANES = 128
+SUBLANES = 8
 BF16 = jnp.bfloat16
 F32 = jnp.float32
 PARAMS = pltpu.CompilerParams(
@@ -92,11 +93,26 @@
         edges[1][0] = rows[tokens - cols :]
 
 
+def pack_kernel(half, deep, w_ref, out_ref):
+    height, width = out_ref.shape
+    at = lax.broadcasted_iota(jnp.int32, (height, 1), 0) + pl.program_id(0) * height
+    rows = jnp.where(at < deep, w_ref[...], jnp.zeros((), BF16))
+    for k in range(width // (2 * LANES)):
+        for side in range(2):
+            first, end = k * LANES, min((k + 1) * LANES, half)
+            piece = rows[:, side * half + first : side * half + end]
+            if end - first < LANES:
+                blank = jnp.zeros((height, LANES - (end - first)), BF16)
+                piece = jnp.concatenate([piece, blank], axis=1)
+            out_ref[:, (2 * k + side) * LANES : (2 * k + side + 1) * LANES] = piece
+
+
 def ffn_kernel(frames, rows, cols, halos, place, x_ref, *refs):
     halo = refs[:halos]
-    wv, wg, cv, cg, bv, bg, out, xs, left, mid, right = refs[halos:]
+    w_ref, taps, bias, out, xs, upa, upb, laid = refs[halos:]
     own = frames * rows * cols
     edge = frames * cols
+    per = cols // SUBLANES
 
     @pl.when(pl.program_id(0) == 0)
     def _():
@@ -104,42 +120,100 @@
         for k in range(halos):
             xs[own + k * edge : own + (k + 1) * edge] = halo[k][...]
 
-    total = own + halos * edge
-    at = lax.rem(lax.broadcasted_iota(jnp.int32, (total, 1), 0), cols)
-    first, last = at == 0, at == cols - 1
-    above_ok = place[0] > 0
-    for side, (w, c, b) in enumerate(((wv, cv, bv), (wg, cg, bg))):
-        up = jnp.dot(xs[...], w[...], preferred_element_type=F32).astype(BF16).astype(F32)
-        mid[side] = up
-        left[side] = jnp.where(first, 0.0, pltpu.roll(up, 1, 0))
-        right[side] = jnp.where(last, 0.0, pltpu.roll(up, total - 1, 0))
-
-    def row_of(side, f, r):
+    has_above = place[0] > 0
+    spot = lax.broadcasted_iota(jnp.int32, (SUBLANES, LANES), 0)
+
+    def product(k, up):
+        both = jnp.dot(
+            xs[...], w_ref[:, 2 * k * LANES : 2 * (k + 1) * LANES], preferred_element_type=F32
+        )
+        up[0] = both[:, :LANES]
+        up[1] = both[:, LANES:]
+
+    def row_of(up, side, f, r):
         if 0 <= r < rows:
-            at = slice((f * rows + r) * cols, (f * rows + r + 1) * cols)
-            return [ref[side, at] for ref in (left, mid, right)]
-        if halos == 1:
-            at = slice(own + f * cols, own + (f + 1) * cols)
-            used = above_ok if r < 0 else jnp.logical_not(above_ok)
-            return [jnp.where(used, ref[side, at], 0.0) for ref in (left, mid, right)]
-        start = own + (0 if r < 0 else edge) + f * cols
-        at = slice(start, start + cols)
-        return [ref[side, at] for ref in (left, mid, right)]
-
-    for f in range(frames):
-        for r in range(rows):
-            convs = []
-            for side, (c, b) in enumerate(((cv, bv), (cg, bg))):
-                total_row = jnp.broadcast_to(b[...], (cols, b.shape[1]))
-                for above in range(3):
-                    three = row_of(side, f, r + above - 1)
-                    for across in range(3):
-                        k = above * 3 + across
-                        total_row = total_row + c[k : k + 1] * three[across]
-                convs.append(total_row)
-            value, gate = convs
-            at = slice((f * rows + r) * cols, (f * rows + r + 1) * cols)
-            out[at] = (value * (gate * (1.0 / (1.0 + jnp.exp(-gate))))).astype(BF16)
+            first, used = (f * rows + r) * cols, None
+        elif halos == 1:
+            first = own + f * cols
+            used = has_above if r < 0 else jnp.logical_not(has_above)
+        else:
+            first, used = own + (0 if r < 0 else edge) + f * cols, None
+        row = [up[side, pl.ds(first + i, SUBLANES, stride=per), :] for i in range(per)]
+        return row if used is None else [jnp.where(used, part, 0.0) for part in row]
+
+    def conv(k, up):
+        for f in range(frames):
+            for r in range(rows):
+                pair = []
+                for side in range(2):
+                    lanes = slice((2 * k + side) * LANES, (2 * k + side + 1) * LANES)
+                    three = [row_of(up, side, f, r + a) for a in (-1, 0, 1)]
+                    left, mid, right = (
+                        [
+                            sum(
+                                taps[3 * a + b : 3 * a + b + 1, lanes] * three[a][i]
+                                for a in range(3)
+                            )
+                            for i in range(per)
+                        ]
+                        for b in range(3)
+                    )
+                    before = jnp.where(spot == 0, 0.0, pltpu.roll(left[per - 1], 1, 0))
+                    after = jnp.where(
+                        spot == SUBLANES - 1, 0.0, pltpu.roll(right[0], SUBLANES - 1, 0)
+                    )
+                    left = [before] + left[: per - 1]
+                    right = right[1:] + [after]
+                    pair.append(
+                        [bias[:, lanes] + mid[i] + left[i] + right[i] for i in range(per)]
+                    )
+                first = (f * rows + r) * cols
+                for i in range(per):
+                    half = 0.5 * pair[1][i]
+                    laid[k, pl.ds(first + i, SUBLANES, stride=per), :] = pair[0][i] * (
+                        half + half * jnp.tanh(half)
+                    )
+                out[first : first + cols, k * LANES : (k + 1) * LANES] = laid[
+                    k, first : first + cols
+                ].astype(BF16)
+
+    product(0, upa)
+    product(1, upb)
+    conv(0, upa)
+    conv(1, upb)
+
+
+def earlier(totals, peers):
+    me = lax.axis_index("tm")
+    rows = totals.shape[0]
+
+    def swap(array, bit):
+        pairs = [(i, i ^ bit) for i in range(peers)]
+        return lax.ppermute(array.astype(BF16), "tm", pairs).astype(F32)
+
+    def joined(mine, other, upper):
+        both = jnp.stack([jnp.where(upper, other, mine), jnp.where(upper, mine, other)])
+        return both.reshape((-1,) + mine.shape[1:])
+
+    odd, second = lax.rem(me, 2) == 1, lax.rem(me // 2, 2) == 1
+    near = swap(totals, 1)
+    pair = (totals + near).reshape(2, rows // 2, -1)
+    pair = jnp.where(odd, pair[1], pair[0])
+    next_pair = swap(pair, 2)
+    four = (pair + next_pair).reshape(2, rows // 4, -1)
+    running = jnp.where(second, four[1], four[0])
+    prior = jnp.zeros_like(running)
+    step = 4
+    while step < peers:
+        got = lax.ppermute(
+            running.astype(BF16), "tm", [(i, i + step) for i in range(peers - step)]
+        ).astype(F32)
+        prior, running = prior + got, running + got
+        step *= 2
+    prior = joined(prior, swap(prior, 2), second)
+    prior = prior + jnp.where(second, next_pair, 0.0)
+    prior = joined(prior, swap(prior, 1), odd)
+    return prior + jnp.where(odd, near, 0.0)
 
 
 def local(
@@ -163,8 +237,7 @@
     peers = lax.axis_size("tm")
     each = heads // parts
     half = w_up.shape[1] // 2
-    block = 2 * LANES
-    half_pad = up_to(half, block)
+    half_pad = up_to(half, 2 * LANES)
     deep = w_up.shape[0]
     deep_pad = up_to(deep, 8)
     depth = peers * deep_pad
@@ -173,14 +246,25 @@
     def round_space(array, k):
         return lax.ppermute(array, "space", [(i, (i + k) % parts) for i in range(parts)])
 
-    def filled(array):
-        side = jnp.zeros(array.shape[:-1] + (half_pad - half,), array.dtype)
-        return jnp.concatenate([array[..., :half], side, array[..., half:], side], axis=-1)
-
-    weights = jnp.pad(filled(w_up), ((0, deep_pad - deep), (0, 0)))
+    def interleaved(array):
+        both = array.reshape(array.shape[0], 2, half)
+        both = jnp.pad(both, ((0, 0), (0, 0), (0, half_pad - half)))
+        both = both.reshape(array.shape[0], 2, half_pad // LANES, LANES)
+        return both.transpose(0, 2, 1, 3).reshape(array.shape[0], 2 * half_pad)
+
+    height = 48 if deep_pad % 48 == 0 else deep_pad
+    weights = pl.pallas_call(
+        functools.partial(pack_kernel, half, deep),
+        grid=(deep_pad // height,),
+        in_specs=[pl.BlockSpec((height, 2 * half), lambda i: (i, 0))],
+        out_specs=pl.BlockSpec((height, 2 * half_pad), lambda i: (i, 0)),
+        out_shape=jax.ShapeDtypeStruct((deep_pad, 2 * half_pad), BF16),
+        compiler_params=PARAMS,
+        name="pack",
+    )(w_up)
     weights = lax.all_gather(weights, "tm", axis=0).reshape(depth, 2 * half_pad)
-    taps = filled(conv_weight.reshape(9, 2 * half))
-    bias = filled(conv_bias.reshape(1, 2 * half))
+    taps = interleaved(conv_weight.reshape(9, 2 * half))
+    bias = interleaved(conv_bias.reshape(1, 2 * half))
 
     def frame_block(*shape):
         return pl.BlockSpec((1,) + shape, lambda f, _: (f,) + (0,) * len(shape))
@@ -206,16 +290,8 @@
     mine = sums[0].astype(F32)
     for k in range(1, parts):
         mine = mine + round_space(sums[k], k).astype(F32)
-    running = jnp.sum(mine, axis=0)
-    prior = jnp.zeros_like(running)
-    step = 1
-    while step < peers:
-        got = lax.ppermute(
-            running.astype(BF16), "tm", [(i, i + step) for i in range(peers - step)]
-        ).astype(F32)
-        prior = prior + got
-        running = running + got
-        step *= 2
+    prior = earlier(jnp.sum(mine, axis=0).reshape(each * head_size, LANES), peers)
+    prior = prior.reshape(part_shape)
     states = (prior + jnp.cumsum(mine, axis=0)).astype(BF16)
     gathered = [states] + [round_space(states, k) for k in range(1, parts)]
     start = jnp.concatenate(
@@ -260,25 +336,24 @@
             lax.ppermute(edges[1], "space", [(i, i + 1) for i in range(parts - 1)]),
             lax.ppermute(edges[0], "space", [(i + 1, i) for i in range(parts - 1)]),
         ]
-    blocks = half_pad // block
     own = frames * tokens
     total = own + halos * frames * cols
 
-    def column(height, shift):
-        return pl.BlockSpec((height, block), lambda j, _: (0, j + shift))
+    def column(rows_in, wide):
+        return pl.BlockSpec((rows_in, wide), lambda j, _: (0, j))
 
     hidden = pl.pallas_call(
         functools.partial(ffn_kernel, frames, rows, cols, halos),
         grid_spec=pltpu.PrefetchScalarGridSpec(
             num_scalar_prefetch=1,
-            grid=(blocks,),
+            grid=(half_pad // (2 * LANES),),
             in_specs=[whole(own, depth)]
             + [whole(frames * cols, depth)] * halos
-            + [column(depth, 0), column(depth, blocks)]
-            + [column(9, 0), column(9, blocks), column(1, 0), column(1, blocks)],
-            out_specs=column(own, 0),
+            + [column(depth, 4 * LANES), column(9, 4 * LANES), column(1, 4 * LANES)],
+            out_specs=column(own, 2 * LANES),
             scratch_shapes=[pltpu.VMEM((total, depth), BF16)]
-            + [pltpu.VMEM((2, total, block), F32)] * 3,
+            + [pltpu.VMEM((2, total, LANES), F32)] * 2
+            + [pltpu.VMEM((2, own, LANES), F32)],
         ),
         out_shape=jax.ShapeDtypeStruct((own, half), BF16),
         compiler_params=PARAMS,
@@ -288,10 +363,7 @@
         x.reshape(own, depth),
         *[a.reshape(frames * cols, depth) for a in around],
         weights,
-        weights,
         taps,
-        taps,
-        bias,
         bias,
     )
     return mixed.reshape(stream.shape), hidden.reshape(frames, rows, cols, half)

time: 211 us -> 186 us (0.88)
  waiting for transfers between devices: 113 us -> 86.8 us
  local copies, waits for them, and re-layouts: 8.82 us -> 5.92 us
    ppermute x4 -> x6, waiting for transfers between devices: 48 us -> 19.7 us  [the longest x2 9.95 us: earlier(): lax.ppermute(running.astype(BF16), 'tm', [(i, i + step) for i in range(pe...]
    ppermute x3, waiting for transfers between devices: 24.1 us -> 28.9 us  [round_space(): lax.ppermute(array, 'space', [(i, (i + k) % parts) for i in range(parts)])]
    pallas_call x0 -> x1, Pallas kernels: none -> 3.65 us  [local(): pl.pallas_call(functools.partial(pack_kernel, half, deep), grid=(deep_pad...]
    pallas_call x1, Pallas kernels: 31.7 us -> 28.6 us  [local(): pl.pallas_call(functools.partial(ffn_kernel, frames, rows, cols, halos),...]
    all_gather x1, waiting for transfers between devices: 40.7 us -> 38.2 us  [local(): weights = lax.all_gather(weights, 'tm', axis=0).reshape(depth, 2 * half_pad)]
    concatenate x3 -> x0, local copies, waits for them, and re-layouts: 2.52 us -> none  [filled(): jnp.concatenate([array[..., :half], side, array[..., half:], side], axis=-1)]
    ppermute x4 -> x6, starting transfers between devices: 12.2 us -> 14.2 us  [the longest x2 8.16 us: earlier(): lax.ppermute(running.astype(BF16), 'tm', [(i, i + step) for i in range(pe...]
  transfers between devices with their start and end apart: 8 -> 10, of which waited for: 8 -> 10; matrix products, arithmetic and copies ran while one was open for 3% -> 4% of each run, Pallas kernels for 11% -> 13%
where the time goes in v2:
time: 186 us; the launch traced here: 184 us
  waiting for transfers between devices  86.8 us (47%)
  Pallas kernels  55.5 us (30%)
  starting transfers between devices  18.1 us (10%)
  between operations  14.2 us (8%)
  local copies, waits for them, and re-layouts  5.92 us (3%)
  other arithmetic  3.37 us (2%)
    all_gather x1, waiting for transfers between devices, local(): weights = lax.all_gather(weights, 'tm', axis=0).reshape(depth, 2 * half_pad)  38.2 us
    ppermute x3, waiting for transfers between devices, round_space(): lax.ppermute(array, 'space', [(i, (i + k) % parts) for i in range(parts)])  28.9 us
    pallas_call x1, Pallas kernels, local(): pl.pallas_call(functools.partial(ffn_kernel, frames, rows, cols, halos),...  28.6 us
    pallas_call x1, Pallas kernels, local(): pl.pallas_call(functools.partial(attn_kernel, heads, head_size, parts, de...  16 us
    ppermute x2, waiting for transfers between devices, earlier(): lax.ppermute(running.astype(BF16), 'tm', [(i, i + step) for i in range(pe...  9.95 us
    ppermute x4, waiting for transfers between devices, swap(): return lax.ppermute(array.astype(BF16), 'tm', pairs).astype(F32)  9.77 us
    ppermute x2, starting transfers between devices, earlier(): lax.ppermute(running.astype(BF16), 'tm', [(i, i + step) for i in range(pe...  8.16 us
    pallas_call x1, Pallas kernels, local(): pl.pallas_call(functools.partial(kv_kernel, heads, head_size, parts), gri...  7.26 us
  transfers between devices with their start and end apart: 10, of which 10 were waited for; matrix products, arithmetic and copies ran while one was open for 4% of the time, Pallas kernels for 13%

profile of v2, /device:TPU:19, one launch (start us, length us, event | category | flops | bytes accessed | tf_op | source)
XLA Modules:
  0.0 183.9 jit_solution(11584178064178718192)
XLA Ops:
  7.2 3.7 %pack.1 = bf16[144,5632]{1,0:T(8,128)(2,1)} custom-call(bf16[140,5600]{1,0:T(8,128)(2,1)} %w_ref.1), custom_call_target="tpu_custom_call" | custom-call | tf_op jit(solution)/shard_map/pack/pallas_call | solution.py:256
  10.9 7.3 %frame_sums.1 = (bf16[2,10,112,128]{3,2,1,0:T(8,128)(2,1)}, bf16[2,10,112,128]{3,2,1,0:T(8,128)(2,1)}) custom-call(s32[1]{0:T(128)} %bitcast.place, bf16[2,240,2240]{2,1,0:T(8,128)(2,1)} %bitcast.43, bf16[2,240,2240]{2,1,0:T(8,128)(2,1)} %bitcast.44), custom_call_target="tpu_custom_call" | custom-call | tf_op jit(solution)/shard_map/frame_sums/pallas_call | solution.py:277
  18.2 1.3 collective-permute-start
  19.4 12.9 %collective-permute-done = bf16[2,10,112,128]{3,2,1,0:T(8,128)(2,1)S(1)} collective-permute-done((bf16[2,10,112,128]{3,2,1,0:T(8,128)(2,1)}, bf16[2,10,112,128]{3,2,1,0:T(8,128)(2,1)S(1)}, u32[]{:S(2)}, u32[]{:S(2)}) %collective-permute-start) | collective-permute-done | bytes 573472 | tf_op jit(solution)/shard_map/ppermute | solution.py:247
  32.3 1.3 fusion.1
  33.6 1.5 collective-permute-start.1
  35.1 1.3 collective-permute-done.1
  37.0 4.7 %collective-permute-done.2 = bf16[560,128]{1,0:T(8,128)(2,1)S(1)} collective-permute-done((bf16[560,128]{1,0:T(8,128)(2,1)S(1)}, bf16[560,128]{1,0:T(8,128)(2,1)S(1)}, u32[]{:S(2)}, u32[]{:S(2)}) %collective-permute-start.2) | collective-permute-done | bytes 143392 | tf_op jit(solution)/shard_map/ppermute | solution.py:192
  41.7 6.9 %collective-permute-start.3 = (bf16[280,128]{1,0:T(8,128)(2,1)S(1)}, bf16[280,128]{1,0:T(8,128)(2,1)S(1)}, u32[]{:S(2)}, u32[]{:S(2)}) collective-permute-start(bf16[280,128]{1,0:T(8,128)(2,1)S(1)} %fusion.12), channel_id=1, source_target_pairs={{0,8},{2,10},{4,12},{6,14},{8,16},{10,18},{12,20},{14,22},{16,24},... | collective-permute-start | bytes 215048 | tf_op jit(solution)/shard_map/ppermute | solution.py:208
  48.6 3.2 %collective-permute-done.3 = bf16[280,128]{1,0:T(8,128)(2,1)S(1)} collective-permute-done((bf16[280,128]{1,0:T(8,128)(2,1)S(1)}, bf16[280,128]{1,0:T(8,128)(2,1)S(1)}, u32[]{:S(2)}, u32[]{:S(2)}) %collective-permute-start.3) | collective-permute-done | bytes 71712 | tf_op jit(solution)/shard_map/ppermute | solution.py:208
  51.9 1.3 collective-permute-start.4
  53.2 6.7 %collective-permute-done.4 = bf16[280,128]{1,0:T(8,128)(2,1)S(1)} collective-permute-done((bf16[280,128]{1,0:T(8,128)(2,1)S(1)}, bf16[280,128]{1,0:T(8,128)(2,1)S(1)}, u32[]{:S(2)}, u32[]{:S(2)}) %collective-permute-start.4) | collective-permute-done | bytes 71712 | tf_op jit(solution)/shard_map/ppermute | solution.py:208
  60.7 2.8 %collective-permute-done.5 = bf16[280,128]{1,0:T(8,128)(2,1)S(1)} collective-permute-done((bf16[280,128]{1,0:T(8,128)(2,1)S(1)}, bf16[280,128]{1,0:T(8,128)(2,1)S(1)}, u32[]{:S(2)}, u32[]{:S(2)}) %collective-permute-start.5) | collective-permute-done | bytes 71712 | tf_op jit(solution)/shard_map/ppermute | solution.py:192
  63.7 3.3 %collective-permute-start.6 = (bf16[560,128]{1,0:T(8,128)(2,1)S(1)}, bf16[560,128]{1,0:T(8,128)(2,1)S(1)}, u32[]{:S(2)}, u32[]{:S(2)}) collective-permute-start(bf16[560,128]{1,0:T(8,128)(2,1)S(1)} %fusion.11), channel_id=1, source_target_pairs={{0,2},{2,0},{4,6},{6,4},{8,10},{10,8},{12,14},{14,12},{16,18},{18,... | collective-permute-start | bytes 430088 | tf_op jit(solution)/shard_map/ppermute | solution.py:192
  67.0 1.0 collective-permute-done.6
  68.2 1.1 copy-done
  69.5 1.3 collective-permute-start.7
  73.0 1.4 pad_maximum_fusion.in_ref
  74.4 9.6 %collective-permute-done.7.refs_1_ = bf16[2,10,112,128]{3,2,1,0:T(8,128)(2,1)S(1)} collective-permute-done((bf16[2,10,112,128]{3,2,1,0:T(8,128)(2,1)S(1)}, bf16[2,10,112,128]{3,2,1,0:T(8,128)(2,1)S(1)}, u32[]{:S(2)}, u32[]{:S(2)}) %collective-permute-start.7) | collective-permute-done | bytes 573472 | tf_op jit(solution)/shard_map/ppermute | solution.py:247
  84.7 16.0 %attention.1 = (bf16[2,240,2240]{2,1,0:T(8,128)(2,1)}, bf16[2,240,2304]{2,1,0:T(8,128)(2,1)}, bf16[2,40,2304]{2,1,0:T(8,128)(2,1)}) custom-call(s32[1]{0:T(128)} %bitcast.place, bf16[2,240,2240]{2,1,0:T(8,128)(2,1)} %bitcast.45, bf16[2,240,2240]{2,1,0:T(8,128)(2,1)} %bitcast.46, f32[20,112,128]{2,1,0:T(8,128)} %pad_maximum_fusion.in_ref, ...), custom_call_target="tpu_custom_call" | custom-call | tf_op jit(solution)/shard_map/attention/pallas_call | solution.py:302
  100.7 1.2 collective-permute-start.8
  103.8 6.4 %collective-permute-done.8 = bf16[2,40,2304]{2,1,0:T(8,128)(2,1)S(1)} collective-permute-done((bf16[2,40,2304]{2,1,0:T(8,128)(2,1)}, bf16[2,40,2304]{2,1,0:T(8,128)(2,1)S(1)}, u32[]{:S(2)}, u32[]{:S(2)}) %collective-permute-start.8) | collective-permute-done | bytes 368672 | tf_op jit(solution)/shard_map/ppermute | solution.py:247
  110.2 38.2 %all-gather.3.cloned.1.call-done.refs_1_ = bf16[2304,5632]{1,0:T(8,128)(2,1)} async-done(((bf16[144,5632]{1,0:T(8,128)(2,1)}), bf16[2304,5632]{1,0:T(8,128)(2,1)}) %all-gather.3.cloned.1.call-update) | async-done | bytes 25952272 | tf_op jit(solution)/shard_map/all_gather | solution.py:265
  148.4 28.6 %mix_ffn.1 = bf16[480,2800]{1,0:T(8,128)(2,1)} custom-call(s32[1]{0:T(128)} %bitcast.place, bf16[480,2304]{1,0:T(8,128)(2,1)} %bitcast.42, bf16[80,2304]{1,0:T(8,128)(2,1)} %bitcast.47, bf16[2304,5632]{1,0:T(8,128)(2,1)} %all-gather.3.cloned.1.call-done.refs_1_, f32[9,5632]{1,0:T(8,128)} %reshape.92.refs_2_, f32[1,5632]{1,0:T(1,128)} %bitcast.48), custom_call_target="tpu_custom_call" | custom-call | tf_op jit(solution)/shard_map/mix_ffn/pallas_call | solution.py:345
  (48 shorter events, 6.9 us)
Async XLA Ops:
  7.2 141.2 %all-gather.3.cloned.1.call-start = ((), (), s32[]{:S(2)}) async-start(), calls=%async_computation | async-start | bytes 27574272 | tf_op jit(solution)/shard_map/all_gather | solution.py:265
  18.2 14.2 %collective-permute-start = (bf16[2,10,112,128]{3,2,1,0:T(8,128)(2,1)}, bf16[2,10,112,128]{3,2,1,0:T(8,128)(2,1)S(1)}, u32[]{:S(2)}, u32[]{:S(2)}) collective-permute-start(bf16[2,10,112,128]{3,2,1,0:T(8,128)(2,1)} %get-tuple-element.8), channel_id=1, source_target_pairs={{0,1},{1,0},{2,3},{3,2},{4,5},{5,4},{6,7},{7,6},{8,9},{9,8},{10,11... | collective-permute-start | bytes 1720328 | tf_op jit(solution)/shard_map/ppermute | solution.py:247
  33.6 2.8 %collective-permute-start.1 = (bf16[1120,128]{1,0:T(8,128)(2,1)S(1)}, bf16[1120,128]{1,0:T(8,128)(2,1)S(1)}, u32[]{:S(2)}, u32[]{:S(2)}) collective-permute-start(bf16[1120,128]{1,0:T(8,128)(2,1)S(1)} %bitcast_convert_fusion), channel_id=1, source_target_pairs={{0,2},{2,0},{4,6},{6,4},{8,10},{10,8},{12,14},{14,12},{16,18},{18,... | collective-permute-start | bytes 860168 | tf_op jit(solution)/shard_map/ppermute | solution.py:192
  36.5 5.2 %collective-permute-start.2 = (bf16[560,128]{1,0:T(8,128)(2,1)S(1)}, bf16[560,128]{1,0:T(8,128)(2,1)S(1)}, u32[]{:S(2)}, u32[]{:S(2)}) collective-permute-start(bf16[560,128]{1,0:T(8,128)(2,1)S(1)} %fusion.10), channel_id=1, source_target_pairs={{0,4},{2,6},{4,0},{6,2},{8,12},{10,14},{12,8},{14,10},{16,20},{18,... | collective-permute-start | bytes 430088 | tf_op jit(solution)/shard_map/ppermute | solution.py:192
  41.7 10.1 %collective-permute-start.3 = (bf16[280,128]{1,0:T(8,128)(2,1)S(1)}, bf16[280,128]{1,0:T(8,128)(2,1)S(1)}, u32[]{:S(2)}, u32[]{:S(2)}) collective-permute-start(bf16[280,128]{1,0:T(8,128)(2,1)S(1)} %fusion.12), channel_id=1, source_target_pairs={{0,8},{2,10},{4,12},{6,14},{8,16},{10,18},{12,20},{14,22},{16,24},... | collective-permute-start | bytes 215048 | tf_op jit(solution)/shard_map/ppermute | solution.py:208
  51.9 8.0 %collective-permute-start.4 = (bf16[280,128]{1,0:T(8,128)(2,1)S(1)}, bf16[280,128]{1,0:T(8,128)(2,1)S(1)}, u32[]{:S(2)}, u32[]{:S(2)}) collective-permute-start(bf16[280,128]{1,0:T(8,128)(2,1)S(1)} %fusion.6), channel_id=1, source_target_pairs={{0,16},{2,18},{4,20},{6,22},{8,24},{10,26},{12,28},{14,30},{1,17},... | collective-permute-start | bytes 215048 | tf_op jit(solution)/shard_map/ppermute | solution.py:208
  59.9 3.6 %collective-permute-start.5 = (bf16[280,128]{1,0:T(8,128)(2,1)S(1)}, bf16[280,128]{1,0:T(8,128)(2,1)S(1)}, u32[]{:S(2)}, u32[]{:S(2)}) collective-permute-start(bf16[280,128]{1,0:T(8,128)(2,1)S(1)} %fusion.9), channel_id=1, source_target_pairs={{0,4},{2,6},{4,0},{6,2},{8,12},{10,14},{12,8},{14,10},{16,20},{18,... | collective-permute-start | bytes 215048 | tf_op jit(solution)/shard_map/ppermute | solution.py:192
  63.7 4.3 %collective-permute-start.6 = (bf16[560,128]{1,0:T(8,128)(2,1)S(1)}, bf16[560,128]{1,0:T(8,128)(2,1)S(1)}, u32[]{:S(2)}, u32[]{:S(2)}) collective-permute-start(bf16[560,128]{1,0:T(8,128)(2,1)S(1)} %fusion.11), channel_id=1, source_target_pairs={{0,2},{2,0},{4,6},{6,4},{8,10},{10,8},{12,14},{14,12},{16,18},{18,... | collective-permute-start | bytes 430088 | tf_op jit(solution)/shard_map/ppermute | solution.py:192
  68.0 1.2 copy-start
  69.2 1.6 copy-start.8
  69.2 2.2 %copy-start.9 = (f32[2240]{0:T(1024)S(1)}, f32[2240]{0:T(1024)}, u32[]{:S(2)}) copy-start(f32[2240]{0:T(1024)} %param.19) | copy-start | bytes 26884
  69.2 2.8 %copy-start.10 = (f32[2240]{0:T(1024)S(1)}, f32[2240]{0:T(1024)}, u32[]{:S(2)}) copy-start(f32[2240]{0:T(1024)} %param.20) | copy-start | bytes 26884
  69.2 3.4 %copy-start.7 = (f32[20,112]{1,0:T(8,128)S(1)}, f32[20,112]{1,0:T(8,128)}, u32[]{:S(2)}) copy-start(f32[20,112]{1,0:T(8,128)} %param.17) | copy-start | bytes 26884
  69.4 4.9 %copy-start.1 = (bf16[2,10,112,128]{3,2,1,0:T(8,128)(2,1)}, bf16[2,10,112,128]{3,2,1,0:T(8,128)(2,1)S(1)}, u32[]{:S(2)}) copy-start(bf16[2,10,112,128]{3,2,1,0:T(8,128)(2,1)S(1)} %add_convert_fusion.refs_0_) | copy-start | bytes 1720324
  69.5 3.5 %copy-start.2 = (f32[20,112,112]{2,1,0:T(8,128)S(1)}, f32[20,112,112]{2,1,0:T(8,128)}, u32[]{:S(2)}) copy-start(f32[20,112,112]{2,1,0:T(8,128)} %param.16) | copy-start | bytes 3010564
  69.5 14.5 %collective-permute-start.7 = (bf16[2,10,112,128]{3,2,1,0:T(8,128)(2,1)S(1)}, bf16[2,10,112,128]{3,2,1,0:T(8,128)(2,1)S(1)}, u32[]{:S(2)}, u32[]{:S(2)}) collective-permute-start(bf16[2,10,112,128]{3,2,1,0:T(8,128)(2,1)S(1)} %add_convert_fusion.refs_0_), channel_id=1, source_target_pairs={{0,1},{1,0},{2,3},{3,2},{4,5},{5,4},{6,7},{7,6},{8,9},{9,8},{10,11... | collective-permute-start | bytes 1720328 | tf_op jit(solution)/shard_map/ppermute | solution.py:247
  83.9 0.8 copy-start.3
  84.7 17.2 %copy-start.6 = (f32[5600]{0:T(1024)S(1)}, f32[5600]{0:T(1024)}, u32[]{:S(2)}) copy-start(f32[5600]{0:T(1024)} %param.23) | copy-start | bytes 67204
  84.7 17.3 %copy-start.5 = (f32[3,3,5600]{2,1,0:T(4,128)S(1)}, f32[3,3,5600]{2,1,0:T(4,128)}, u32[]{:S(2)}) copy-start(f32[3,3,5600]{2,1,0:T(4,128)} %param.22) | copy-start | bytes 604804
  100.7 9.5 %collective-permute-start.8 = (bf16[2,40,2304]{2,1,0:T(8,128)(2,1)}, bf16[2,40,2304]{2,1,0:T(8,128)(2,1)S(1)}, u32[]{:S(2)}, u32[]{:S(2)}) collective-permute-start(bf16[2,40,2304]{2,1,0:T(8,128)(2,1)} %get-tuple-element.11), channel_id=1, source_target_pairs={{0,1},{1,0},{2,3},{3,2},{4,5},{5,4},{6,7},{7,6},{8,9},{9,8},{10,11... | collective-permute-start | bytes 1105928 | tf_op jit(solution)/shard_map/ppermute | solution.py:247
  110.2 38.2 %copy-start.4 = (bf16[2,40,2304]{2,1,0:T(8,128)(2,1)}, bf16[2,40,2304]{2,1,0:T(8,128)(2,1)S(1)}, u32[]{:S(2)}) copy-start(bf16[2,40,2304]{2,1,0:T(8,128)(2,1)S(1)} %collective-permute-done.8) | copy-start | bytes 1105924
Sparse Core Ops, SparseCore 0:
  11.0 137.3 all-gather.2

commit v3 on v2

--- a/solution.py
+++ b/solution.py
@@ -108,27 +108,25 @@
 
 
 def ffn_kernel(frames, rows, cols, halos, place, x_ref, *refs):
-    halo = refs[:halos]
-    w_ref, taps, bias, out, xs, upa, upb, laid = refs[halos:]
+    w_ref, taps, bias, out, upa, upb, rawa, rawb, laid = refs
     own = frames * rows * cols
     edge = frames * cols
     per = cols // SUBLANES
 
-    @pl.when(pl.program_id(0) == 0)
-    def _():
-        xs[:own] = x_ref[...]
-        for k in range(halos):
-            xs[own + k * edge : own + (k + 1) * edge] = halo[k][...]
-
     has_above = place[0] > 0
     spot = lax.broadcasted_iota(jnp.int32, (SUBLANES, LANES), 0)
 
-    def product(k, up):
+    def product(k, up, raw):
         both = jnp.dot(
-            xs[...], w_ref[:, 2 * k * LANES : 2 * (k + 1) * LANES], preferred_element_type=F32
+            x_ref[...], w_ref[:, 2 * k * LANES : 2 * (k + 1) * LANES], preferred_element_type=F32
         )
-        up[0] = both[:, :LANES]
-        up[1] = both[:, LANES:]
+        raw[0] = both[:, :LANES]
+        raw[1] = both[:, LANES:]
+        for side in range(2):
+            for first in range(0, both.shape[0], cols):
+                for i in range(per):
+                    at = slice(first + i * SUBLANES, first + (i + 1) * SUBLANES)
+                    up[side, at] = raw[side, pl.ds(first + i, SUBLANES, stride=per), :]
 
     def row_of(up, side, f, r):
         if 0 <= r < rows:
@@ -138,7 +136,9 @@
             used = has_above if r < 0 else jnp.logical_not(has_above)
         else:
             first, used = own + (0 if r < 0 else edge) + f * cols, None
-        row = [up[side, pl.ds(first + i, SUBLANES, stride=per), :] for i in range(per)]
+        row = [
+            up[side, first + i * SUBLANES : first + (i + 1) * SUBLANES] for i in range(per)
+        ]
         return row if used is None else [jnp.where(used, part, 0.0) for part in row]
 
     def conv(k, up):
@@ -169,7 +169,7 @@
                     )
                 first = (f * rows + r) * cols
                 for i in range(per):
-                    half = 0.5 * pair[1][i]
+                    half = pair[1][i]
                     laid[k, pl.ds(first + i, SUBLANES, stride=per), :] = pair[0][i] * (
                         half + half * jnp.tanh(half)
                     )
@@ -177,8 +177,8 @@
                     k, first : first + cols
                 ].astype(BF16)
 
-    product(0, upa)
-    product(1, upb)
+    product(0, upa, rawa)
+    product(1, upb, rawb)
     conv(0, upa)
     conv(1, upb)
 
@@ -248,6 +248,7 @@
 
     def interleaved(array):
         both = array.reshape(array.shape[0], 2, half)
+        both = jnp.concatenate([both[:, :1], 0.5 * both[:, 1:]], axis=1)
         both = jnp.pad(both, ((0, 0), (0, 0), (0, half_pad - half)))
         both = both.reshape(array.shape[0], 2, half_pad // LANES, LANES)
         return both.transpose(0, 2, 1, 3).reshape(array.shape[0], 2 * half_pad)
@@ -339,6 +340,10 @@
     own = frames * tokens
     total = own + halos * frames * cols
 
+    joined = jnp.concatenate(
+        [x.reshape(own, depth)] + [a.reshape(frames * cols, depth) for a in around]
+    )
+
     def column(rows_in, wide):
         return pl.BlockSpec((rows_in, wide), lambda j, _: (0, j))
 
@@ -347,12 +352,10 @@
         grid_spec=pltpu.PrefetchScalarGridSpec(
             num_scalar_prefetch=1,
             grid=(half_pad // (2 * LANES),),
-            in_specs=[whole(own, depth)]
-            + [whole(frames * cols, depth)] * halos
+            in_specs=[pl.BlockSpec(memory_space=pltpu.VMEM)]
             + [column(depth, 4 * LANES), column(9, 4 * LANES), column(1, 4 * LANES)],
             out_specs=column(own, 2 * LANES),
-            scratch_shapes=[pltpu.VMEM((total, depth), BF16)]
-            + [pltpu.VMEM((2, total, LANES), F32)] * 2
+            scratch_shapes=[pltpu.VMEM((2, total, LANES), F32)] * 4
             + [pltpu.VMEM((2, own, LANES), F32)],
         ),
         out_shape=jax.ShapeDtypeStruct((own, half), BF16),
@@ -360,8 +363,7 @@
         name="mix_ffn",
     )(
         place,
-        x.reshape(own, depth),
-        *[a.reshape(frames * cols, depth) for a in around],
+        joined,
         weights,
         taps,
         bias,

time: 186 us -> 185 us (level)
  other arithmetic: 3.37 us -> 7.62 us
  waiting for transfers between devices: 86.8 us -> 83.3 us
    all_gather x1, waiting for transfers between devices: 38.2 us -> 32 us  [local(): weights = lax.all_gather(weights, 'tm', axis=0).reshape(depth, 2 * half_pad)]
    ppermute x3, waiting for transfers between devices: 28.9 us -> 32.9 us  [round_space(): lax.ppermute(array, 'space', [(i, (i + k) % parts) for i in range(parts)])]
    concatenate x0 -> x2, other arithmetic: none -> 3.9 us  [the longest x1 3.27 us: local(): jnp.concatenate([x.reshape(own, depth)] + [a.reshape(frames * cols, depth...]
  transfers between devices with their start and end apart: 10 -> 10, of which waited for: 10 -> 9; matrix products, arithmetic and copies ran while one was open for 4% -> 6% of each run, Pallas kernels for 13% -> 13%
where the time goes in v3:
time: 185 us; the launch traced here: 183 us
  waiting for transfers between devices  83.3 us (45%)
  Pallas kernels  54.1 us (29%)
  starting transfers between devices  18.3 us (10%)
  between operations  14.2 us (8%)
  other arithmetic  7.62 us (4%)
  local copies, waits for them, and re-layouts  5.13 us (3%)
    ppermute x3, waiting for transfers between devices, round_space(): lax.ppermute(array, 'space', [(i, (i + k) % parts) for i in range(parts)])  32.9 us
    all_gather x1, waiting for transfers between devices, local(): weights = lax.all_gather(weights, 'tm', axis=0).reshape(depth, 2 * half_pad)  32 us
    pallas_call x1, Pallas kernels, local(): pl.pallas_call(functools.partial(ffn_kernel, frames, rows, cols, halos),...  27.4 us
    pallas_call x1, Pallas kernels, local(): pl.pallas_call(functools.partial(attn_kernel, heads, head_size, parts, de...  15.7 us
    ppermute x2, waiting for transfers between devices, earlier(): lax.ppermute(running.astype(BF16), 'tm', [(i, i + step) for i in range(pe...  9.95 us
    ppermute x4, waiting for transfers between devices, swap(): return lax.ppermute(array.astype(BF16), 'tm', pairs).astype(F32)  8.48 us
    ppermute x2, starting transfers between devices, earlier(): lax.ppermute(running.astype(BF16), 'tm', [(i, i + step) for i in range(pe...  8.28 us
    pallas_call x1, Pallas kernels, local(): pl.pallas_call(functools.partial(kv_kernel, heads, head_size, parts), gri...  7.26 us
  transfers between devices with their start and end apart: 10, of which 9 were waited for; matrix products, arithmetic and copies ran while one was open for 6% of the time, Pallas kernels for 13%

profile of v3, /device:TPU:19, one launch (start us, length us, event | category | flops | bytes accessed | tf_op | source)
XLA Modules:
  0.0 182.7 jit_solution(11301583061250071847)
XLA Ops:
  7.2 3.7 %pack.1 = bf16[144,5632]{1,0:T(8,128)(2,1)} custom-call(bf16[140,5600]{1,0:T(8,128)(2,1)} %w_ref.1), custom_call_target="tpu_custom_call" | custom-call | tf_op jit(solution)/shard_map/pack/pallas_call | solution.py:257
  10.9 7.3 %frame_sums.1 = (bf16[2,10,112,128]{3,2,1,0:T(8,128)(2,1)}, bf16[2,10,112,128]{3,2,1,0:T(8,128)(2,1)}) custom-call(s32[1]{0:T(128)} %bitcast.place, bf16[2,240,2240]{2,1,0:T(8,128)(2,1)} %bitcast.43, bf16[2,240,2240]{2,1,0:T(8,128)(2,1)} %bitcast.44), custom_call_target="tpu_custom_call" | custom-call | tf_op jit(solution)/shard_map/frame_sums/pallas_call | solution.py:278
  18.2 1.3 collective-permute-start
  19.4 12.9 %collective-permute-done = bf16[2,10,112,128]{3,2,1,0:T(8,128)(2,1)S(1)} collective-permute-done((bf16[2,10,112,128]{3,2,1,0:T(8,128)(2,1)}, bf16[2,10,112,128]{3,2,1,0:T(8,128)(2,1)S(1)}, u32[]{:S(2)}, u32[]{:S(2)}) %collective-permute-start) | collective-permute-done | bytes 573472 | tf_op jit(solution)/shard_map/ppermute | solution.py:247
  32.3 1.3 fusion.1
  33.7 1.5 collective-permute-start.1
  35.2 1.3 collective-permute-done.1
  37.0 4.7 %collective-permute-done.2 = bf16[560,128]{1,0:T(8,128)(2,1)S(1)} collective-permute-done((bf16[560,128]{1,0:T(8,128)(2,1)S(1)}, bf16[560,128]{1,0:T(8,128)(2,1)S(1)}, u32[]{:S(2)}, u32[]{:S(2)}) %collective-permute-start.2) | collective-permute-done | bytes 143392 | tf_op jit(solution)/shard_map/ppermute | solution.py:192
  41.8 7.0 %collective-permute-start.3 = (bf16[280,128]{1,0:T(8,128)(2,1)S(1)}, bf16[280,128]{1,0:T(8,128)(2,1)S(1)}, u32[]{:S(2)}, u32[]{:S(2)}) collective-permute-start(bf16[280,128]{1,0:T(8,128)(2,1)S(1)} %fusion.13), channel_id=1, source_target_pairs={{0,8},{2,10},{4,12},{6,14},{8,16},{10,18},{12,20},{14,22},{16,24},... | collective-permute-start | bytes 215048 | tf_op jit(solution)/shard_map/ppermute | solution.py:208
  48.8 3.2 %collective-permute-done.3 = bf16[280,128]{1,0:T(8,128)(2,1)S(1)} collective-permute-done((bf16[280,128]{1,0:T(8,128)(2,1)S(1)}, bf16[280,128]{1,0:T(8,128)(2,1)S(1)}, u32[]{:S(2)}, u32[]{:S(2)}) %collective-permute-start.3) | collective-permute-done | bytes 71712 | tf_op jit(solution)/shard_map/ppermute | solution.py:208
  52.1 1.3 collective-permute-start.4
  53.4 6.7 %collective-permute-done.4 = bf16[280,128]{1,0:T(8,128)(2,1)S(1)} collective-permute-done((bf16[280,128]{1,0:T(8,128)(2,1)S(1)}, bf16[280,128]{1,0:T(8,128)(2,1)S(1)}, u32[]{:S(2)}, u32[]{:S(2)}) %collective-permute-start.4) | collective-permute-done | bytes 71712 | tf_op jit(solution)/shard_map/ppermute | solution.py:208
  61.2 2.5 %collective-permute-done.5 = bf16[280,128]{1,0:T(8,128)(2,1)S(1)} collective-permute-done((bf16[280,128]{1,0:T(8,128)(2,1)S(1)}, bf16[280,128]{1,0:T(8,128)(2,1)S(1)}, u32[]{:S(2)}, u32[]{:S(2)}) %collective-permute-start.5) | collective-permute-done | bytes 71712 | tf_op jit(solution)/shard_map/ppermute | solution.py:192
  63.9 3.3 %collective-permute-start.6 = (bf16[560,128]{1,0:T(8,128)(2,1)S(1)}, bf16[560,128]{1,0:T(8,128)(2,1)S(1)}, u32[]{:S(2)}, u32[]{:S(2)}) collective-permute-start(bf16[560,128]{1,0:T(8,128)(2,1)S(1)} %fusion.12), channel_id=1, source_target_pairs={{0,2},{2,0},{4,6},{6,4},{8,10},{10,8},{12,14},{14,12},{16,18},{18,... | collective-permute-start | bytes 430088 | tf_op jit(solution)/shard_map/ppermute | solution.py:192
  69.6 1.4 pad_maximum_fusion.1.in_ref
  72.3 1.3 collective-permute-start.7
  73.6 13.3 %collective-permute-done.7.refs_1_ = bf16[2,10,112,128]{3,2,1,0:T(8,128)(2,1)S(1)} collective-permute-done((bf16[2,10,112,128]{3,2,1,0:T(8,128)(2,1)S(1)}, bf16[2,10,112,128]{3,2,1,0:T(8,128)(2,1)S(1)}, u32[]{:S(2)}, u32[]{:S(2)}) %collective-permute-start.7) | collective-permute-done | bytes 573472 | tf_op jit(solution)/shard_map/ppermute | solution.py:247
  87.8 15.7 %attention.1 = (bf16[2,240,2240]{2,1,0:T(8,128)(2,1)}, bf16[2,240,2304]{2,1,0:T(8,128)(2,1)}, bf16[2,40,2304]{2,1,0:T(8,128)(2,1)}) custom-call(s32[1]{0:T(128)} %bitcast.place, bf16[2,240,2240]{2,1,0:T(8,128)(2,1)} %bitcast.45, bf16[2,240,2240]{2,1,0:T(8,128)(2,1)} %bitcast.46, f32[20,112,128]{2,1,0:T(8,128)} %pad_maximum_fusion.1.in_ref, ...), custom_call_target="tpu_custom_call" | custom-call | tf_op jit(solution)/shard_map/attention/pallas_call | solution.py:303
  103.5 1.3 collective-permute-start.8
  105.0 0.9 reshape.92.refs_1_
  106.5 6.7 %collective-permute-done.8 = bf16[2,40,2304]{2,1,0:T(8,128)(2,1)S(1)} collective-permute-done((bf16[2,40,2304]{2,1,0:T(8,128)(2,1)}, bf16[2,40,2304]{2,1,0:T(8,128)(2,1)S(1)}, u32[]{:S(2)}, u32[]{:S(2)}) %collective-permute-start.8) | collective-permute-done | bytes 368672 | tf_op jit(solution)/shard_map/ppermute | solution.py:247
  113.2 3.3 %pad_maximum_fusion.x_ref = bf16[560,2304]{1,0:T(8,128)(2,1)} fusion(bf16[80,2304]{1,0:T(8,128)(2,1)S(1)} %bitcast.47, bf16[480,2304]{1,0:T(8,128)(2,1)} %bitcast.42), kind=kLoop, calls=%fused_computation | loop fusion | flops 5160960 | bytes 5160960 | tf_op jit(solution)/shard_map/concatenate | solution.py:343
  116.4 32.0 %all-gather.3.cloned.1.call-done.refs_0_ = bf16[2304,5632]{1,0:T(8,128)(2,1)} async-done(((bf16[144,5632]{1,0:T(8,128)(2,1)}), bf16[2304,5632]{1,0:T(8,128)(2,1)}) %all-gather.3.cloned.1.call-update) | async-done | bytes 25952272 | tf_op jit(solution)/shard_map/all_gather | solution.py:266
  148.4 27.4 %mix_ffn.1 = bf16[480,2800]{1,0:T(8,128)(2,1)} custom-call(s32[1]{0:T(128)} %bitcast.place, bf16[560,2304]{1,0:T(8,128)(2,1)} %pad_maximum_fusion.x_ref, bf16[2304,5632]{1,0:T(8,128)(2,1)} %all-gather.3.cloned.1.call-done.refs_0_, f32[9,5632]{1,0:T(8,128)} %reshape.92.refs_1_, f32[1,5632]{1,0:T(1,128)} %bitcast.48), custom_call_target="tpu_custom_call" | custom-call | tf_op jit(solution)/shard_map/mix_ffn/pallas_call | solution.py:350
  (49 shorter events, 7.3 us)
Async XLA Ops:
  7.2 141.3 %all-gather.3.cloned.1.call-start = ((), (), s32[]{:S(2)}) async-start(), calls=%async_computation | async-start | bytes 27574272 | tf_op jit(solution)/shard_map/all_gather | solution.py:266
  18.2 14.2 %collective-permute-start = (bf16[2,10,112,128]{3,2,1,0:T(8,128)(2,1)}, bf16[2,10,112,128]{3,2,1,0:T(8,128)(2,1)S(1)}, u32[]{:S(2)}, u32[]{:S(2)}) collective-permute-start(bf16[2,10,112,128]{3,2,1,0:T(8,128)(2,1)} %get-tuple-element.8), channel_id=1, source_target_pairs={{0,1},{1,0},{2,3},{3,2},{4,5},{5,4},{6,7},{7,6},{8,9},{9,8},{10,11... | collective-permute-start | bytes 1720328 | tf_op jit(solution)/shard_map/ppermute | solution.py:247
  33.7 2.8 %collective-permute-start.1 = (bf16[1120,128]{1,0:T(8,128)(2,1)S(1)}, bf16[1120,128]{1,0:T(8,128)(2,1)S(1)}, u32[]{:S(2)}, u32[]{:S(2)}) collective-permute-start(bf16[1120,128]{1,0:T(8,128)(2,1)S(1)} %bitcast_convert_fusion), channel_id=1, source_target_pairs={{0,2},{2,0},{4,6},{6,4},{8,10},{10,8},{12,14},{14,12},{16,18},{18,... | collective-permute-start | bytes 860168 | tf_op jit(solution)/shard_map/ppermute | solution.py:192
  35.2 25.8 %copy-start.4 = (f32[3,3,5600]{2,1,0:T(4,128)S(1)}, f32[3,3,5600]{2,1,0:T(4,128)}, u32[]{:S(2)}) copy-start(f32[3,3,5600]{2,1,0:T(4,128)} %param.22) | copy-start | bytes 604804
  36.5 5.2 %collective-permute-start.2 = (bf16[560,128]{1,0:T(8,128)(2,1)S(1)}, bf16[560,128]{1,0:T(8,128)(2,1)S(1)}, u32[]{:S(2)}, u32[]{:S(2)}) collective-permute-start(bf16[560,128]{1,0:T(8,128)(2,1)S(1)} %fusion.11), channel_id=1, source_target_pairs={{0,4},{2,6},{4,0},{6,2},{8,12},{10,14},{12,8},{14,10},{16,20},{18,... | collective-permute-start | bytes 430088 | tf_op jit(solution)/shard_map/ppermute | solution.py:192
  41.8 25.5 %copy-start.7 = (f32[2240]{0:T(1024)S(1)}, f32[2240]{0:T(1024)}, u32[]{:S(2)}) copy-start(f32[2240]{0:T(1024)} %param.18) | copy-start | bytes 26884
  41.8 26.1 %copy-start.8 = (f32[2240]{0:T(1024)S(1)}, f32[2240]{0:T(1024)}, u32[]{:S(2)}) copy-start(f32[2240]{0:T(1024)} %param.19) | copy-start | bytes 26884
  41.8 26.7 %copy-start.9 = (f32[2240]{0:T(1024)S(1)}, f32[2240]{0:T(1024)}, u32[]{:S(2)}) copy-start(f32[2240]{0:T(1024)} %param.20) | copy-start | bytes 26884
  41.8 27.3 %copy-start.5 = (f32[5600]{0:T(1024)S(1)}, f32[5600]{0:T(1024)}, u32[]{:S(2)}) copy-start(f32[5600]{0:T(1024)} %param.23) | copy-start | bytes 67204
  41.8 27.4 %copy-start.6 = (f32[20,112]{1,0:T(8,128)S(1)}, f32[20,112]{1,0:T(8,128)}, u32[]{:S(2)}) copy-start(f32[20,112]{1,0:T(8,128)} %param.17) | copy-start | bytes 26884
  41.8 10.2 %collective-permute-start.3 = (bf16[280,128]{1,0:T(8,128)(2,1)S(1)}, bf16[280,128]{1,0:T(8,128)(2,1)S(1)}, u32[]{:S(2)}, u32[]{:S(2)}) collective-permute-start(bf16[280,128]{1,0:T(8,128)(2,1)S(1)} %fusion.13), channel_id=1, source_target_pairs={{0,8},{2,10},{4,12},{6,14},{8,16},{10,18},{12,20},{14,22},{16,24},... | collective-permute-start | bytes 215048 | tf_op jit(solution)/shard_map/ppermute | solution.py:208
  52.1 8.0 %collective-permute-start.4 = (bf16[280,128]{1,0:T(8,128)(2,1)S(1)}, bf16[280,128]{1,0:T(8,128)(2,1)S(1)}, u32[]{:S(2)}, u32[]{:S(2)}) collective-permute-start(bf16[280,128]{1,0:T(8,128)(2,1)S(1)} %fusion.7), channel_id=1, source_target_pairs={{0,16},{2,18},{4,20},{6,22},{8,24},{10,26},{12,28},{14,30},{1,17},... | collective-permute-start | bytes 215048 | tf_op jit(solution)/shard_map/ppermute | solution.py:208
  60.1 3.6 %collective-permute-start.5 = (bf16[280,128]{1,0:T(8,128)(2,1)S(1)}, bf16[280,128]{1,0:T(8,128)(2,1)S(1)}, u32[]{:S(2)}, u32[]{:S(2)}) collective-permute-start(bf16[280,128]{1,0:T(8,128)(2,1)S(1)} %fusion.10), channel_id=1, source_target_pairs={{0,4},{2,6},{4,0},{6,2},{8,12},{10,14},{12,8},{14,10},{16,20},{18,... | collective-permute-start | bytes 215048 | tf_op jit(solution)/shard_map/ppermute | solution.py:192
  61.2 8.4 %copy-start.2 = (f32[20,112,112]{2,1,0:T(8,128)S(1)}, f32[20,112,112]{2,1,0:T(8,128)}, u32[]{:S(2)}) copy-start(f32[20,112,112]{2,1,0:T(8,128)} %param.16) | copy-start | bytes 3010564
  63.9 7.1 %collective-permute-start.6 = (bf16[560,128]{1,0:T(8,128)(2,1)S(1)}, bf16[560,128]{1,0:T(8,128)(2,1)S(1)}, u32[]{:S(2)}, u32[]{:S(2)}) collective-permute-start(bf16[560,128]{1,0:T(8,128)(2,1)S(1)} %fusion.12), channel_id=1, source_target_pairs={{0,2},{2,0},{4,6},{6,4},{8,10},{10,8},{12,14},{14,12},{16,18},{18,... | collective-permute-start | bytes 430088 | tf_op jit(solution)/shard_map/ppermute | solution.py:192
  71.0 1.1 copy-start
  72.3 14.7 %copy-start.1 = (bf16[2,10,112,128]{3,2,1,0:T(8,128)(2,1)}, bf16[2,10,112,128]{3,2,1,0:T(8,128)(2,1)S(1)}, u32[]{:S(2)}) copy-start(bf16[2,10,112,128]{3,2,1,0:T(8,128)(2,1)S(1)} %add_convert_fusion.refs_0_) | copy-start | bytes 1720324
  72.3 14.7 %collective-permute-start.7 = (bf16[2,10,112,128]{3,2,1,0:T(8,128)(2,1)S(1)}, bf16[2,10,112,128]{3,2,1,0:T(8,128)(2,1)S(1)}, u32[]{:S(2)}, u32[]{:S(2)}) collective-permute-start(bf16[2,10,112,128]{3,2,1,0:T(8,128)(2,1)S(1)} %add_convert_fusion.refs_0_), channel_id=1, source_target_pairs={{0,1},{1,0},{2,3},{3,2},{4,5},{5,4},{6,7},{7,6},{8,9},{9,8},{10,11... | collective-permute-start | bytes 1720328 | tf_op jit(solution)/shard_map/ppermute | solution.py:247
  86.9 0.8 copy-start.3
  103.5 9.7 %collective-permute-start.8 = (bf16[2,40,2304]{2,1,0:T(8,128)(2,1)}, bf16[2,40,2304]{2,1,0:T(8,128)(2,1)S(1)}, u32[]{:S(2)}, u32[]{:S(2)}) collective-permute-start(bf16[2,40,2304]{2,1,0:T(8,128)(2,1)} %get-tuple-element.11), channel_id=1, source_target_pairs={{0,1},{1,0},{2,3},{3,2},{4,5},{5,4},{6,7},{7,6},{8,9},{9,8},{10,11... | collective-permute-start | bytes 1105928 | tf_op jit(solution)/shard_map/ppermute | solution.py:247
Sparse Core Ops, SparseCore 0:
  11.0 137.3 all-gather.2
